TPU v7x, 128 devices: a whole 4x4x4 slice. The times are simulated.
128 devices in a mesh: leaf: 4 (over y), prow: 4 (over z), pcol: 8 (over x, core).
Axes of the slice: x: 4, y: 4, z: 4, core: 2. Of those that a mesh axis runs over, the one named last changes fastest.
Arguments:
- front_pivot: float32 [4, 1536, 1536], P('leaf', ('prow', 'pcol')), as said below
- front_lower: float32 [4, 6144, 1536], P('leaf', ('prow', 'pcol')), may hold values from -0.375 to 0.375
- front_rest: float32 [4, 6144, 6144], P('leaf', ('prow', 'pcol')), as said below
- parent_front: float32 [4, 8192, 4096], P('leaf', ('prow', 'pcol')), may hold values from -1.3 to 4.4, as said below
- relation: int32 [4, 6144], replicated, may hold values from 0 to 8191, as said below
Outputs:
- factor_pivot: float32 [4, 1536, 1536], P('leaf', ('prow', 'pcol'))
- factor_lower: float32 [4, 6144, 1536], P('leaf', ('prow', 'pcol'))
- parent_out: float32 [4, 8192, 4096], P('leaf', ('prow', 'pcol'))
Inputs may be any that keep to these rules, and one draw needn't show every extreme that they name: Each front_pivot[g] is symmetric positive definite, with no eigenvalue under 0.3. Each front_rest[g] is symmetric, with diagonal entries between 6 and 9 and small off-diagonal entries. `parent_front`: the two column halves of one parent front together form a symmetric matrix. `relation`: for every front and every k, the entries k * 192 to (k + 1) * 192 - 1 rise strictly and lie in k * 256 to (k + 1) * 256 - 1, and take both ends of that range.
All inputs are finite; a program needn't handle non-finite values.
Results may differ from a plain program's by a relative error of at most 0.0029.
Values may be sent and summed in bfloat16 or wider, within the bound.
A program may use at most 128 MiB of HBM per device.

v0:
```python
import jax
import jax.numpy as jnp
from jax import lax
from jax.sharding import PartitionSpec as P

PW = 512


highest = lax.Precision.HIGHEST


def from_partner(value, axis, apart):
    mask = 2**apart
    pairs = [(source, source ^ mask) for source in range(lax.axis_size(axis))]
    return lax.ppermute(value, axis, pairs)


def factor_blocked(matrix):
    block_order = matrix.shape[0]
    if block_order <= 128:
        factor = jnp.linalg.cholesky(matrix)
        identity = jnp.eye(block_order, dtype=jnp.float32)
        inverse = lax.linalg.triangular_solve(factor, identity, left_side=True, lower=True)
        return (factor, inverse)
    middle = block_order // 2
    top_factor, top_inverse = factor_blocked(matrix[:middle, :middle])
    lower_block = jnp.dot(matrix[middle:, :middle], top_inverse.T, precision=highest)
    reduced = matrix[middle:, middle:] - jnp.dot(lower_block, lower_block.T, precision=highest)
    bottom_factor, bottom_inverse = factor_blocked(reduced)
    mixed_inverse = -jnp.dot(
        bottom_inverse, jnp.dot(lower_block, top_inverse, precision=highest), precision=highest
    )
    upper_zeros = jnp.zeros((middle, block_order - middle), jnp.float32)
    factor = jnp.concatenate(
        [
            jnp.concatenate([top_factor, upper_zeros], axis=1),
            jnp.concatenate([lower_block, bottom_factor], axis=1),
        ],
        axis=0,
    )
    inverse = jnp.concatenate(
        [
            jnp.concatenate([top_inverse, upper_zeros], axis=1),
            jnp.concatenate([mixed_inverse, bottom_inverse], axis=1),
        ],
        axis=0,
    )
    return (factor, inverse)


def local(front_pivot, front_lower, front_rest, parent_front, relation):
    position = lax.axis_index(("prow", "pcol"))
    pivot_rows = front_pivot[0]
    lower_rows = front_lower[0]
    pivot_order = pivot_rows.shape[1]
    rows_here = pivot_rows.shape[0]
    for panel_idx in range(pivot_order // PW):
        first_col = panel_idx * PW
        after_col = first_col + PW
        column = lax.all_gather(
            pivot_rows[:, first_col:after_col], ("prow", "pcol"), axis=0, tiled=True
        )
        corner, corner_inverse = factor_blocked(column[first_col:after_col])
        trailing = jnp.dot(column[after_col:], corner_inverse.T, precision=highest)
        full_panel = jnp.concatenate(
            [jnp.zeros((first_col, PW), jnp.float32), corner, trailing], axis=0
        )
        own_panel = lax.dynamic_slice_in_dim(full_panel, position * rows_here, rows_here, 0)
        lower_panel = jnp.dot(
            lower_rows[:, first_col:after_col], corner_inverse.T, precision=highest
        )
        pivot_rows = pivot_rows.at[:, first_col:after_col].set(own_panel)
        lower_rows = lower_rows.at[:, first_col:after_col].set(lower_panel)
        if after_col < pivot_order:
            pivot_rows = pivot_rows.at[:, after_col:].add(
                -jnp.dot(own_panel, trailing.T, precision=highest)
            )
            lower_rows = lower_rows.at[:, after_col:].add(
                -jnp.dot(lower_panel, trailing.T, precision=highest)
            )
    shared = lower_rows.astype(jnp.bfloat16)
    rest_rows = front_rest[0]
    block_rows = rest_rows.shape[0]
    child_order = rest_rows.shape[1]
    update = jnp.einsum(
        "ik,jk->ij",
        shared,
        lax.all_gather(shared, ("prow", "pcol"), axis=0, tiled=True),
        preferred_element_type=jnp.float32,
    )
    schur_rows = rest_rows - update
    leaf_index = lax.axis_index("leaf")
    side_bit = leaf_index % 2
    partner = leaf_index + 1 - 2 * side_bit
    child_half = child_order // 2
    window = parent_front.shape[1]
    parent_half = parent_front.shape[2]
    blocks = child_half // block_rows
    kept_cols = lax.dynamic_slice_in_dim(schur_rows, side_bit * child_half, child_half, 1)
    sent_cols = lax.dynamic_slice_in_dim(schur_rows, (1 - side_bit) * child_half, child_half, 1)
    received = from_partner(sent_cols.astype(jnp.bfloat16), "leaf", 0).astype(sent_cols.dtype)
    window_iota = jnp.arange(window, dtype=jnp.int32)
    block_starts = jnp.arange(blocks, dtype=jnp.int32) * window

    def spread(values, child_idx):
        link_map = lax.dynamic_index_in_dim(relation, child_idx, 0, keepdims=False)
        row_links = (
            lax.dynamic_slice_in_dim(link_map, position * block_rows, block_rows, 0)
            - position * window
        )
        col_links = (
            lax.dynamic_slice_in_dim(link_map, side_bit * child_half, child_half, 0)
            - side_bit * parent_half
        )
        col_local = col_links.reshape(blocks, block_rows) - block_starts[:, None]
        row_table = (window_iota[:, None] == row_links[None, :]).astype(jnp.float32)
        col_table = (col_local[:, :, None] == window_iota[None, None, :]).astype(jnp.float32)
        placed = jnp.einsum(
            "akb,kbj->akj",
            values.reshape(block_rows, blocks, block_rows),
            col_table,
            precision=highest,
        )
        return jnp.dot(row_table, placed.reshape(block_rows, blocks * window), precision=highest)

    merged = parent_front[0] + spread(kept_cols, leaf_index) + spread(received, partner)
    return (pivot_rows[None], lower_rows[None], merged[None])


def solution(mesh):
    return jax.shard_map(
        local,
        mesh=mesh,
        in_specs=(
            P("leaf", ("prow", "pcol"), None),
            P("leaf", ("prow", "pcol"), None),
            P("leaf", ("prow", "pcol"), None),
            P("leaf", ("prow", "pcol"), None),
            P(),
        ),
        out_specs=(
            P("leaf", ("prow", "pcol"), None),
            P("leaf", ("prow", "pcol"), None),
            P("leaf", ("prow", "pcol"), None),
        ),
        check_vma=False,
    )
```

profile of v0, /device:TPU:1, one launch (start us, length us, event | category | flops | bytes accessed | tf_op | source)
XLA Modules:
  0.0 639.1 jit_solution(9453721911537562738)
XLA Ops:
  10.5 48.9 %all-gather.5.cloned.1.call-done = f32[1536,512]{1,0:T(8,128)} async-done(((f32[48,512]{1,0:T(8,128)}), f32[1536,512]{1,0:T(8,128)}) %all-gather.5.cloned.1.call-update) | async-done | bytes 3145744 | tf_op jit(solution)/shard_map/all_gather | solution.py:60
  61.2 11.7 %cholesky.194 = f32[128,128]{1,0:T(8,128)S(1)} custom-call(f32[128,128]{1,0:T(8,128)S(1)} %get-tuple-element.166), custom_call_target="Cholesky" | custom-call | tf_op jit(solution)/shard_map/jit(cholesky)/cholesky | solution.py:21
  74.2 9.8 %custom-call.16 = f32[1,128,128]{1,2,0:T(8,128)S(1)} custom-call(f32[1,128,128]{2,1,0:T(8,128)S(1)} %get-tuple-element.159), custom_call_target="InvertDiagBlocksLowerTriangular" | custom-call | tf_op jit(solution)/shard_map/triangular_solve/custom-call.0 | solution.py:23
  86.3 11.7 %cholesky.205 = f32[128,128]{1,0:T(8,128)S(1)} custom-call(f32[128,128]{1,0:T(8,128)S(1)} %fusion.139), custom_call_target="Cholesky" | custom-call | tf_op jit(solution)/shard_map/jit(cholesky)/cholesky | solution.py:21
  99.3 10.0 %custom-call.17 = f32[1,128,128]{1,2,0:T(8,128)S(1)} custom-call(f32[1,128,128]{2,1,0:T(8,128)S(1)} %get-tuple-element.157), custom_call_target="InvertDiagBlocksLowerTriangular" | custom-call | tf_op jit(solution)/shard_map/triangular_solve/custom-call.0 | solution.py:23
  113.9 11.7 %cholesky.216 = f32[128,128]{1,0:T(8,128)S(1)} custom-call(f32[128,128]{1,0:T(8,128)S(1)} %fusion.137), custom_call_target="Cholesky" | custom-call | tf_op jit(solution)/shard_map/jit(cholesky)/cholesky | solution.py:21
  127.0 9.8 %custom-call.18 = f32[1,128,128]{1,2,0:T(8,128)S(1)} custom-call(f32[1,128,128]{2,1,0:T(8,128)S(1)} %get-tuple-element.155), custom_call_target="InvertDiagBlocksLowerTriangular" | custom-call | tf_op jit(solution)/shard_map/triangular_solve/custom-call.0 | solution.py:23
  138.9 11.9 %cholesky.227 = f32[128,128]{1,0:T(8,128)S(1)} custom-call(f32[128,128]{1,0:T(8,128)S(1)} %fusion.135), custom_call_target="Cholesky" | custom-call | tf_op jit(solution)/shard_map/jit(cholesky)/cholesky | solution.py:21
  178.9 41.7 %all-gather.7.cloned.1.call-done = f32[1536,512]{1,0:T(8,128)} async-done(((f32[48,512]{1,0:T(8,128)}), f32[1536,512]{1,0:T(8,128)}) %all-gather.7.cloned.1.call-update) | async-done | bytes 3145744 | tf_op jit(solution)/shard_map/all_gather | solution.py:60
  222.4 11.7 %cholesky.238 = f32[128,128]{1,0:T(8,128)S(1)} custom-call(f32[128,128]{1,0:T(8,128)S(1)} %get-tuple-element.164), custom_call_target="Cholesky" | custom-call | tf_op jit(solution)/shard_map/jit(cholesky)/cholesky | solution.py:21
  248.1 11.7 %cholesky.249 = f32[128,128]{1,0:T(8,128)S(1)} custom-call(f32[128,128]{1,0:T(8,128)S(1)} %fusion.131), custom_call_target="Cholesky" | custom-call | tf_op jit(solution)/shard_map/jit(cholesky)/cholesky | solution.py:21
  261.7 9.9 %custom-call.21 = f32[1,128,128]{1,2,0:T(8,128)S(1)} custom-call(f32[1,128,128]{2,1,0:T(8,128)S(1)} %get-tuple-element.147), custom_call_target="InvertDiagBlocksLowerTriangular" | custom-call | tf_op jit(solution)/shard_map/triangular_solve/custom-call.0 | solution.py:23
  281.5 13.2 %cholesky.260 = f32[128,128]{1,0:T(8,128)} custom-call(f32[128,128]{1,0:T(8,128)} %fusion.129), custom_call_target="Cholesky" | custom-call | tf_op jit(solution)/shard_map/jit(cholesky)/cholesky | solution.py:21
  298.4 11.3 %custom-call.22 = f32[1,128,128]{1,2,0:T(8,128)} custom-call(f32[1,128,128]{2,1,0:T(8,128)} %get-tuple-element.145), custom_call_target="InvertDiagBlocksLowerTriangular" | custom-call | tf_op jit(solution)/shard_map/triangular_solve/custom-call.0 | solution.py:23
  319.2 11.9 %cholesky.271 = f32[128,128]{1,0:T(8,128)S(1)} custom-call(f32[128,128]{1,0:T(8,128)S(1)} %fusion.127), custom_call_target="Cholesky" | custom-call | tf_op jit(solution)/shard_map/jit(cholesky)/cholesky | solution.py:21
  364.2 33.8 %all-gather.9.cloned.1.call-done = f32[1536,512]{1,0:T(8,128)} async-done(((f32[48,512]{1,0:T(8,128)}), f32[1536,512]{1,0:T(8,128)}) %all-gather.9.cloned.1.call-update) | async-done | bytes 3145744 | tf_op jit(solution)/shard_map/all_gather | solution.py:60
  400.9 11.7 %cholesky.282 = f32[128,128]{1,0:T(8,128)S(1)} custom-call(f32[128,128]{1,0:T(8,128)S(1)} %get-tuple-element.162), custom_call_target="Cholesky" | custom-call | tf_op jit(solution)/shard_map/jit(cholesky)/cholesky | solution.py:21
  425.9 11.9 %cholesky.293 = f32[128,128]{1,0:T(8,128)S(1)} custom-call(f32[128,128]{1,0:T(8,128)S(1)} %fusion.123), custom_call_target="Cholesky" | custom-call | tf_op jit(solution)/shard_map/jit(cholesky)/cholesky | solution.py:21
  451.8 11.7 %cholesky.304 = f32[128,128]{1,0:T(8,128)S(1)} custom-call(f32[128,128]{1,0:T(8,128)S(1)} %fusion.121), custom_call_target="Cholesky" | custom-call | tf_op jit(solution)/shard_map/jit(cholesky)/cholesky | solution.py:21
  464.8 10.0 %custom-call.26 = f32[1,128,128]{1,2,0:T(8,128)S(1)} custom-call(f32[1,128,128]{2,1,0:T(8,128)S(1)} %get-tuple-element.135), custom_call_target="InvertDiagBlocksLowerTriangular" | custom-call | tf_op jit(solution)/shard_map/triangular_solve/custom-call.0 | solution.py:23
  476.6 11.7 %cholesky.315 = f32[128,128]{1,0:T(8,128)S(1)} custom-call(f32[128,128]{1,0:T(8,128)S(1)} %fusion.119), custom_call_target="Cholesky" | custom-call | tf_op jit(solution)/shard_map/jit(cholesky)/cholesky | solution.py:21
  509.7 69.9 %all-gather.11.cloned.1.call-done = bf16[6144,1536]{1,0:T(8,128)(2,1)} async-done(((bf16[192,1536]{1,0:T(8,128)(2,1)}), bf16[6144,1536]{1,0:T(8,128)(2,1)}) %all-gather.11.cloned.1.call-update) | async-done | bytes 18874384 | tf_op jit(solution)/shard_map/all_gather | solution.py:88
  579.6 12.3 %convolution_subtract_fusion = f32[192,6144]{1,0:T(8,128)S(1)} fusion(bf16[192,1536]{1,0:T(8,128)(2,1)S(1)} %copy-done.4, bf16[6144,1536]{1,0:T(8,128)(2,1)} %all-gather.11.cloned.1.call-done, f32[1,192,6144]{2,1,0:T(8,128)} %param.30), kind=kOutput, calls=%fused_computation | convolution fusion | flops 3625058304 | bytes 28901376 | tf_op jit(solution)/shard_map/ik,jk->ij/dot_general | solution.py:85
  609.1 11.5 %collective-permute-done = bf16[192,3072]{1,0:T(8,128)(2,1)} collective-permute-done((bf16[192,3072]{1,0:T(8,128)(2,1)}, bf16[192,3072]{1,0:T(8,128)(2,1)}, u32[]{:S(2)}, u32[]{:S(2)}) %collective-permute-start) | collective-permute-done | bytes 1179680 | tf_op jit(solution)/shard_map/ppermute | solution.py:15
  (271 shorter events, 202.1 us)
Async XLA Ops:
  7.2 52.2 %all-gather.5.cloned.1.call-start = ((), (), s32[]{:S(2)}) async-start(), calls=%async_computation | async-start | bytes 3244032 | tf_op jit(solution)/shard_map/all_gather | solution.py:60
  8.8 211.7 %all-gather.7.cloned.1.call-start = ((), (), s32[]{:S(2)}) async-start(), calls=%async_computation.1 | async-start | bytes 3244032 | tf_op jit(solution)/shard_map/all_gather | solution.py:60
  162.4 7.9 %copy-start.13 = (f32[128,128]{1,0:T(8,128)}, f32[128,128]{1,0:T(8,128)S(1)}, u32[]{:S(2)}) copy-start(f32[128,128]{1,0:T(8,128)S(1)} %copy.169) | copy-start | bytes 196612
  162.7 7.7 %copy-start.11 = (f32[128,128]{1,0:T(8,128)}, f32[128,128]{1,0:T(8,128)S(1)}, u32[]{:S(2)}) copy-start(f32[128,128]{1,0:T(8,128)S(1)} %convolution_negate_fusion.11) | copy-start | bytes 196612
  163.8 6.6 %copy-start.6 = (f32[256,512]{0,1:T(8,128)S(1)}, f32[256,512]{0,1:T(8,128)}, u32[]{:S(2)}) copy-start(f32[256,512]{0,1:T(8,128)} %copy.172) | copy-start | bytes 1572868
  164.6 5.7 copy-start.8
  164.6 5.7 copy-start.9
  165.0 7.1 %copy-start.7 = (f32[256,256]{1,0:T(8,128)}, f32[256,256]{1,0:T(8,128)S(1)}, u32[]{:S(2)}) copy-start(f32[256,256]{1,0:T(8,128)S(1)} %convolution_negate_fusion.4) | copy-start | bytes 786436
  176.2 221.7 %all-gather.9.cloned.1.call-start = ((), (), s32[]{:S(2)}) async-start(), calls=%async_computation.2 | async-start | bytes 3244032 | tf_op jit(solution)/shard_map/all_gather | solution.py:60
  277.8 20.6 %copy-start.10 = (f32[256,256]{0,1:T(8,128)}, f32[256,256]{0,1:T(8,128)S(1)}, u32[]{:S(2)}) copy-start(f32[256,256]{0,1:T(8,128)S(1)} %convolution_subtract_fusion.2) | copy-start | bytes 786436
  343.3 6.8 %copy-start.23 = (f32[128,128]{1,0:T(8,128)}, f32[128,128]{1,0:T(8,128)S(1)}, u32[]{:S(2)}) copy-start(f32[128,128]{1,0:T(8,128)S(1)} %copy.191) | copy-start | bytes 196612
  343.3 6.8 %copy-start.21 = (f32[128,128]{1,0:T(8,128)S(1)}, f32[128,128]{1,0:T(8,128)}, u32[]{:S(2)}) copy-start(f32[128,128]{1,0:T(8,128)} %get-tuple-element.144) | copy-start | bytes 196612
  344.5 7.2 %copy-start.19 = (f32[128,128]{1,0:T(8,128)}, f32[128,128]{1,0:T(8,128)S(1)}, u32[]{:S(2)}) copy-start(f32[128,128]{1,0:T(8,128)S(1)} %convolution_negate_fusion.9) | copy-start | bytes 196612
  346.8 5.0 copy-start.17
  350.1 5.4 copy-start.12
  350.1 5.4 copy-start.14
  353.5 226.0 %all-gather.11.cloned.1.call-start = ((), (), s32[]{:S(2)}) async-start(), calls=%async_computation.3 | async-start | bytes 19464192 | tf_op jit(solution)/shard_map/all_gather | solution.py:88
  357.7 3.5 copy-start.15
  357.7 3.5 copy-start.18
  357.7 3.5 copy-start.20
  357.7 3.5 copy-start.22
  501.6 8.1 %copy-start.1 = (f32[192,1536]{1,0:T(8,128)}, f32[192,1536]{1,0:T(8,128)S(1)}, u32[]{:S(2)}) copy-start(f32[192,1536]{1,0:T(8,128)S(1)} %convolution_dynamic-update-slice_fusion) | copy-start | bytes 3538948
  502.6 77.0 %copy-start.4 = (bf16[192,1536]{1,0:T(8,128)(2,1)S(1)}, bf16[192,1536]{1,0:T(8,128)(2,1)}, u32[]{:S(2)}) copy-start(bf16[192,1536]{1,0:T(8,128)(2,1)} %convert_element_type.48) | copy-start | bytes 1769476
  593.1 27.6 %collective-permute-start = (bf16[192,3072]{1,0:T(8,128)(2,1)}, bf16[192,3072]{1,0:T(8,128)(2,1)}, u32[]{:S(2)}, u32[]{:S(2)}) collective-permute-start(bf16[192,3072]{1,0:T(8,128)(2,1)} %dynamic-slice_convert_fusion), channel_id=1, source_target_pairs={{0,32},{32,0},{64,96},{96,64},{1,33},{33,1},{65,97},{97,65},{2,34}... | collective-permute-start | bytes 3538952 | tf_op jit(solution)/shard_map/ppermute | solution.py:15
  (9 other events, 19.6 us)
Sparse Core Ops, SparseCore 0:
  10.8 48.5 all-gather.4
  176.3 44.2 all-gather.6
  353.7 44.2 all-gather.8
  502.7 76.8 all-gather.10
where the time goes:
time: 650 us; the launch traced here: 639 us
  other arithmetic  305 us (47%)
  waiting for transfers between devices  206 us (32%)
  matrix products  75.3 us (12%)
  local copies, waits for them, and re-layouts  35.4 us (5%)
  between operations  15.6 us (2%)
    another operation x36, other arithmetic, factor_blocked(): factor = jnp.linalg.cholesky(matrix)  152 us
    another operation x24, other arithmetic, factor_blocked(): lax.linalg.triangular_solve(factor, identity, left_side=True, lower=True)  131 us
    all_gather x3, waiting for transfers between devices, local(): lax.all_gather(pivot_rows[:, first_col:after_col], ('prow', 'pcol'), axis...  124 us
    all_gather x1, waiting for transfers between devices, local(): lax.all_gather(shared, ('prow', 'pcol'), axis=0, tiled=True)  69.9 us
  transfers between devices with their start and end apart: 5, of which 5 were waited for; matrix products, arithmetic and copies ran while one was open for 5% of the time, Pallas kernels for 0%

commit v1 on v0

v1 whole, which is shorter than its diff:
```python
import functools

import jax
import jax.numpy as jnp
from jax import lax
from jax.experimental import pallas as pl
from jax.experimental.pallas import tpu as pltpu
from jax.sharding import PartitionSpec as P

DB = 128
PB = 256
f32 = jnp.float32
bf16 = jnp.bfloat16


def two_terms(value):
    high = value.astype(bf16)
    low = (value - high.astype(f32)).astype(bf16)
    return high, low


def nt(a, b):
    return lax.dot_general(a, b, (((1,), (1,)), ((), ())), preferred_element_type=f32)


def nn(a, b):
    return lax.dot_general(a, b, (((1,), (0,)), ((), ())), preferred_element_type=f32)


def left3(value):
    high, low = two_terms(value)
    return jnp.concatenate([high, high, low], axis=1)


def right3(value, axis=1):
    high, low = two_terms(value)
    return jnp.concatenate([high, low, high], axis=axis)


def nt3(a, b):
    return nt(left3(a), right3(b))


def nn3(a, b):
    return nn(left3(a), right3(b, 0))


def factor_corner(work, segments=4):
    count = DB // 8
    sub = lax.broadcasted_iota(jnp.int32, (8, DB), 0)

    def step(first, block, carry):
        start = pl.multiple_of(block * 8, 8)
        rows_d = work[pl.ds(start, 8), :DB]
        rows_e = work[pl.ds(start, 8), DB:]
        lane = jnp.zeros((8, DB), jnp.int32) + start

        def column(rows, k):
            return jnp.take_along_axis(rows, lane + k, axis=1)

        a = {}
        for k in range(8):
            piece = column(rows_d, k)
            for s in range(k, 8):
                a[s, k] = jnp.broadcast_to(piece[s:s + 1], (8, DB))
        r = []
        up = []
        for i in range(8):
            inv = lax.rsqrt(a[i, i])
            r.append(inv)
            for k in range(i + 1, 8):
                a[k, i] = a[k, i] * inv
            for k in range(i + 1, 8):
                for j in range(i + 1, k + 1):
                    a[k, j] = a[k, j] - a[k, i] * a[j, i]
            pair = []
            for side, rows in enumerate((rows_d, rows_e)):
                value = jnp.broadcast_to(rows[i:i + 1], (8, DB))
                for k in range(i):
                    value = value - a[i, k] * up[k][side]
                pair.append(value * inv)
            up.append(pair)
        back = [None] * 8
        for i in reversed(range(8)):
            pair = []
            for side in range(2):
                value = up[i][side]
                for k in range(i + 1, 8):
                    value = value - a[k, i] * back[k][side]
                pair.append(value * r[i])
            back[i] = pair
        for side in range(2):
            value = up[0][side]
            for i in range(1, 8):
                value = jnp.where(sub == i, up[i][side], value)
            work[pl.ds(start, 8), side * DB:(side + 1) * DB] = value
        for v in range(first + 1, count):
            tile_d = work[v * 8:v * 8 + 8, :DB]
            tile_e = work[v * 8:v * 8 + 8, DB:]
            live = jnp.where(v > block, 1.0, 0.0).astype(f32)
            sum_d = sum_e = None
            for k in range(8):
                coef = column(tile_d, k)
                if k == 0:
                    sum_d = coef * back[k][0]
                    sum_e = coef * back[k][1]
                else:
                    sum_d = sum_d + coef * back[k][0]
                    sum_e = sum_e + coef * back[k][1]
            work[v * 8:v * 8 + 8, :DB] = tile_d - live * sum_d
            work[v * 8:v * 8 + 8, DB:] = tile_e - live * sum_e
        return carry

    size = count // segments
    for seg in range(segments):
        lax.fori_loop(seg * size, (seg + 1) * size, lambda b, c, f=seg * size: step(f, b, c), 0)


def factor_kernel(order, rows, where_ref, a_ref, b_ref, l_ref, x_ref, g_ref, m, work, inv, p_hi, p_lo):
    total = order + rows
    eye = (lax.broadcasted_iota(jnp.int32, (DB, DB), 0) == lax.broadcasted_iota(jnp.int32, (DB, DB), 1)).astype(f32)
    low_mask = lax.broadcasted_iota(jnp.int32, (DB, DB), 0) >= lax.broadcasted_iota(jnp.int32, (DB, DB), 1)
    m[:order, :] = a_ref[...]
    m[order:, :] = b_ref[...]
    zero = jnp.zeros((DB, DB), f32)
    for p in range(order // PB):
        c0 = p * PB
        c1 = c0 + DB
        c2 = c0 + PB
        work[:, :DB] = m[c0:c1, c0:c1]
        work[:, DB:] = eye
        factor_corner(work)
        l11 = jnp.where(low_mask, work[:, :DB].T, 0.0)
        i11 = work[:, DB:]
        l21 = nt3(m[c1:c2, c0:c1], i11)
        work[:, :DB] = m[c1:c2, c1:c2] - nt3(l21, l21)
        work[:, DB:] = eye
        factor_corner(work)
        l22 = jnp.where(low_mask, work[:, :DB].T, 0.0)
        i22 = work[:, DB:]
        i21 = -nn3(i22, nn3(l21, i11))
        m[c0:c1, c0:c1] = l11
        m[c0:c1, c1:c2] = zero
        m[c1:c2, c0:c1] = l21
        m[c1:c2, c1:c2] = l22
        inv[c0:c1, :DB] = i11
        inv[c0:c1, DB:] = zero
        inv[c1:c2, :DB] = i21
        inv[c1:c2, DB:] = i22
        panel = nt3(m[c2:, c0:c2], inv[c0:c2, :])
        m[c2:, c0:c2] = panel
        hi, lo = two_terms(panel)
        p_hi[c2:, :] = hi
        p_lo[c2:, :] = lo
        for j in range(c2, order, PB):
            right = jnp.concatenate([p_hi[j:j + PB], p_lo[j:j + PB], p_hi[j:j + PB]], axis=1)
            left = jnp.concatenate([p_hi[j:], p_hi[j:], p_lo[j:]], axis=1)
            m[j:, j:j + PB] = m[j:, j:j + PB] - nt(left, right)
    x_ref[...] = m[order:, :]
    held = l_ref.shape[0]
    top = pl.multiple_of(where_ref[0] * held, 8)
    own = m[pl.ds(top, held), :]
    row_id = lax.broadcasted_iota(jnp.int32, own.shape, 0) + top
    col_id = lax.broadcasted_iota(jnp.int32, own.shape, 1)
    l_ref[...] = jnp.where(col_id <= row_id, own, 0.0)
    for p in reversed(range(order // PB)):
        c0 = p * PB
        c2 = c0 + PB
        rhs = m[order:, c0:c2]
        if c2 < order:
            rhs = rhs - nn3(m[order:, c2:], m[c2:order, c0:c2])
        g = nn3(rhs, inv[c0:c2, :])
        m[order:, c0:c2] = g
        g_ref[:, c0:c2] = g.astype(bf16)


def factor(where, a, b, held):
    order = a.shape[0]
    rows = b.shape[0]
    vm = pl.BlockSpec(memory_space=pltpu.VMEM)
    return pl.pallas_call(
        functools.partial(factor_kernel, order, rows),
        out_shape=(
            jax.ShapeDtypeStruct((held, order), f32),
            jax.ShapeDtypeStruct((rows, order), f32),
            jax.ShapeDtypeStruct((rows, order), bf16),
        ),
        in_specs=[pl.BlockSpec(memory_space=pltpu.SMEM), vm, vm],
        out_specs=(vm, vm, vm),
        scratch_shapes=[
            pltpu.VMEM((order + rows, order), f32),
            pltpu.VMEM((DB, 2 * DB), f32),
            pltpu.VMEM((order, PB), f32),
            pltpu.VMEM((order + rows, PB), bf16),
            pltpu.VMEM((order + rows, PB), bf16),
        ],
        compiler_params=pltpu.CompilerParams(vmem_limit_bytes=60 * 2**20),
        cost_estimate=pl.CostEstimate(flops=100 * 10**9, bytes_accessed=2 * 10**7, transcendentals=0),
        name="factor",
    )(where, a, b)


def assemble_kernel(pick, g_ref, b_ref, c_ref, rows_ref, cols_ref, base_ref, out_ref):
    height = base_ref.shape[0]
    width = base_ref.shape[1]
    schur = c_ref[...].astype(f32) - nt(g_ref[...], b_ref[...])
    high, low = two_terms(schur)
    spot = lax.broadcasted_iota(jnp.int32, (width, high.shape[1]), 0)
    col_table = (spot == cols_ref[0]).astype(bf16)
    spot = lax.broadcasted_iota(jnp.int32, (height, high.shape[0]), 0)
    row_table = (spot == rows_ref[...]).astype(bf16)
    high = nt(high, col_table).astype(bf16)
    low = nt(low, col_table).astype(bf16)
    out_ref[...] = base_ref[...] + (nn(row_table, high) + nn(row_table, low))


def assemble(pick, g, b_all, c, row_link, col_link, base):
    steps, _, wide = col_link.shape
    rows, order = g.shape
    height, full = base.shape
    window = full // steps
    return pl.pallas_call(
        assemble_kernel,
        out_shape=jax.ShapeDtypeStruct(base.shape, f32),
        grid_spec=pltpu.PrefetchScalarGridSpec(
            num_scalar_prefetch=1,
            grid=(steps,),
            in_specs=[
                pl.BlockSpec((rows, order), lambda t, pick: (0, 0)),
                pl.BlockSpec((wide, order), lambda t, pick: (pick[0] + t, 0)),
                pl.BlockSpec((rows, wide), lambda t, pick: (0, pick[1] + t)),
                pl.BlockSpec((1, rows), lambda t, pick: (0, 0)),
                pl.BlockSpec((1, 1, wide), lambda t, pick: (t, 0, 0)),
                pl.BlockSpec((height, window), lambda t, pick: (0, t)),
            ],
            out_specs=pl.BlockSpec((height, window), lambda t, pick: (0, t)),
        ),
        input_output_aliases={6: 0},
        cost_estimate=pl.CostEstimate(flops=5 * 10**9, bytes_accessed=2 * 10**7, transcendentals=0),
        name="assemble",
    )(pick, g, b_all, c, row_link, col_link, base)


AXES = ("leaf", "prow", "pcol")


def local(front_pivot, front_lower, front_rest, parent_front, relation):
    position = lax.axis_index(("prow", "pcol"))
    leaf = lax.axis_index("leaf")
    spots = lax.axis_size("prow") * lax.axis_size("pcol")
    leaves = lax.axis_size("leaf")
    half_spots = spots // 2
    side = leaf % 2
    partner = leaf + 1 - 2 * side
    pivot_rows = front_pivot[0]
    lower_rows = front_lower[0]
    rest_rows = front_rest[0]
    base = parent_front[0]
    rows_here, child_order = rest_rows.shape
    half = child_order // 2
    height, parent_half = base.shape
    steps = 8
    wide = half // steps
    window = parent_half // steps

    matrix = lax.all_gather(pivot_rows, ("prow", "pcol"), axis=0, tiled=True)

    low_bits = lower_rows.astype(bf16)
    swap = []
    mirror = []
    for one in range(leaves):
        for spot in range(spots):
            mirror.append((one * spots + spot, (one ^ 1) * spots + spot))
            if spot // half_spots != one % 2:
                swap.append((one * spots + spot, (one ^ 1) * spots + (spot ^ half_spots)))
    swapped = lax.ppermute(low_bits, AXES, swap)
    block = jnp.where(position // half_spots == side, low_bits, swapped)
    b_all = lax.all_gather(block, ("prow", "pcol"), axis=0, tiled=True)
    other = lax.dynamic_slice_in_dim(rest_rows, (1 - side) * half, half, 1).astype(bf16)
    rest_sib = lax.ppermute(other, AXES, mirror)

    where = jnp.full((1,), position, jnp.int32)
    pivot_out, lower_out, g = factor(where, matrix, lower_rows, pivot_rows.shape[0])
    g_sib = lax.ppermute(g, AXES, mirror)

    def links(child):
        link = lax.dynamic_index_in_dim(relation, child, 0, keepdims=False)
        row_link = lax.dynamic_slice_in_dim(link, position * rows_here, rows_here, 0) - position * height
        col_link = lax.dynamic_slice_in_dim(link, side * half, half, 0) - side * parent_half
        col_link = col_link.reshape(steps, 1, wide) - jnp.arange(steps, dtype=jnp.int32)[:, None, None] * window
        return row_link[None], col_link

    row_own, col_own = links(leaf)
    row_sib, col_sib = links(partner)
    pick_own = jnp.stack([side * steps, side * steps]).astype(jnp.int32)
    pick_sib = jnp.stack([(1 - side) * steps, 0 * side]).astype(jnp.int32)
    merged = assemble(pick_own, g, b_all, rest_rows, row_own, col_own, base)
    merged = assemble(pick_sib, g_sib, b_all, rest_sib, row_sib, col_sib, merged)
    return (pivot_out[None], lower_out[None], merged[None])


def solution(mesh):
    spec = P("leaf", ("prow", "pcol"), None)
    return jax.shard_map(
        local,
        mesh=mesh,
        in_specs=(spec, spec, spec, spec, P()),
        out_specs=(spec, spec, spec),
        check_vma=False,
    )
```

time: 650 us -> 222 us (0.34); the launches traced: 639 us -> 221 us
  other arithmetic: 305 us -> 5.3 us
  waiting for transfers between devices: 206 us -> 38.6 us
  Pallas kernels: 0 us -> 133 us
  matrix products: 75.3 us -> 0 us
  local copies, waits for them, and re-layouts: 35.4 us -> 7.74 us
  starting transfers between devices: 1.77 us -> 21.9 us
    another operation x63 -> x2, other arithmetic: 286 us -> 1.23 us  [the longest x1 0.65 us: local(): pick_sib = jnp.stack([(1 - side) * steps, 0 * side]).astype(jnp.int32)]
    all_gather x4 -> x2, waiting for transfers between devices: 194 us -> 38.5 us  [the longest x1 38.5 us: local(): matrix = lax.all_gather(pivot_rows, ('prow', 'pcol'), axis=0, tiled=True)]
    pallas_call x0 -> x3, Pallas kernels: none -> 133 us  [the longest x1 103 us: factor(): pl.pallas_call(functools.partial(factor_kernel, order, rows), out_shape=(...]
    dot_general x50 -> x0, matrix products: 71.2 us -> none  [the longest x1 12.3 us: local(): jnp.einsum('ik,jk->ij', shared, lax.all_gather(shared, ('prow', 'pcol'),...]
    ppermute x1 -> x3, starting transfers between devices: 1.2 us -> 21.9 us  [the longest x1 20 us: local(): rest_sib = lax.ppermute(other, AXES, mirror)]
    ppermute x1 -> x3, waiting for transfers between devices: 11.5 us -> 0.01 us  [the longest x1 0.01 us: local(): swapped = lax.ppermute(low_bits, AXES, swap)]
    slice x14 -> x0, local copies, waits for them, and re-layouts: 9.13 us -> none  [the longest x9 4.93 us: factor_blocked(): top_factor, top_inverse = factor_blocked(matrix[:middle, :middle])]
    reshape x4 -> x0, local copies, waits for them, and re-layouts: 6.79 us -> none  [the longest x2 6.08 us: spread(): values.reshape(block_rows, blocks, block_rows)]
  transfers between devices with their start and end apart: 5 -> 5, of which waited for: 5 -> 1; matrix products, arithmetic and copies ran while one was open for 5% -> 3% of each run, Pallas kernels for 0% -> 54%
where the time goes in v1:
time: 222 us; the launch traced here: 221 us
  Pallas kernels  133 us (60%)
  waiting for transfers between devices  38.6 us (17%)
  starting transfers between devices  21.9 us (10%)
  between operations  14.2 us (6%)
  local copies, waits for them, and re-layouts  7.74 us (3%)
  other arithmetic  5.3 us (2%)
    pallas_call x1, Pallas kernels, factor(): pl.pallas_call(functools.partial(factor_kernel, order, rows), out_shape=(...  103 us
    all_gather x1, waiting for transfers between devices, local(): matrix = lax.all_gather(pivot_rows, ('prow', 'pcol'), axis=0, tiled=True)  38.5 us
    pallas_call x2, Pallas kernels, assemble(): pl.pallas_call(assemble_kernel, out_shape=jax.ShapeDtypeStruct(base.shape...  30 us
    ppermute x1, starting transfers between devices, local(): rest_sib = lax.ppermute(other, AXES, mirror)  20 us
    unnamed x7, local copies, waits for them, and re-layouts  5.92 us
  transfers between devices with their start and end apart: 5, of which 1 were waited for; matrix products, arithmetic and copies ran while one was open for 3% of the time, Pallas kernels for 54%

profile of v1, /device:TPU:1, one launch (start us, length us, event | category | flops | bytes accessed | tf_op | source)
XLA Modules:
  0.0 221.0 jit_solution(13137197563013567021)
XLA Ops:
  7.2 0.0 copy-start
  7.2 0.0 all-gather.6.cloned.1.call-start
  7.2 4.7 %copy.13 = f32[1,256,4096]{2,1,0:T(8,128)} copy(f32[1,256,4096]{2,1,0:T(8,128)} %param.8) | data formatting | bytes 8388608
  12.0 0.0 all-gather.6.cloned.1.call-update
  12.0 0.0 all-gather.4.cloned.1.call-start
  12.0 0.1 bitcast_convert_fusion
  12.1 0.7 collective-permute-start.1
  12.9 0.0 collective-permute-done.1
  12.9 0.9 broadcast_select_fusion
  13.8 0.0 all-gather.4.cloned.1.call-update
  13.8 1.8 fusion
  15.6 20.0 %collective-permute-start.2 = (bf16[192,3072]{1,0:T(8,128)(2,1)S(1)}, bf16[192,3072]{1,0:T(8,128)(2,1)S(1)}, u32[]{:S(2)}, u32[]{:S(2)}) collective-permute-start(bf16[192,3072]{1,0:T(8,128)(2,1)S(1)} %fusion), channel_id=1, source_target_pairs={{0,32},{1,33},{2,34},{3,35},{4,36},{5,37},{6,38},{7,39},{8,40},{9,... | collective-permute-start | bytes 3538952 | tf_op jit(solution)/shard_map/ppermute | solution.py:280
  35.6 0.6 pad_add_fusion.1.pick
  36.2 1.0 dynamic-slice_subtract_fusion
  37.2 0.7 broadcast_subtract_fusion
  37.8 38.5 %all-gather.6.cloned.1.call-done = f32[1,1536,1536]{2,1,0:T(8,128)} async-done(((f32[1,48,1536]{2,1,0:T(8,128)}), f32[1,1536,1536]{2,1,0:T(8,128)}) %all-gather.6.cloned.1.call-update) | async-done | bytes 9437200 | tf_op jit(solution)/shard_map/all_gather | solution.py:266
  76.4 103.3 %factor.1 = (f32[48,1536]{1,0:T(8,128)}, f32[192,1536]{1,0:T(8,128)}, bf16[192,1536]{1,0:T(8,128)(2,1)}) custom-call(s32[1]{0:T(128)} %bitcast.where_ref, f32[1536,1536]{1,0:T(8,128)} %bitcast.23, f32[192,1536]{1,0:T(8,128)} %bitcast.20), custom_call_target="tpu_custom_call" | custom-call | flops 99999997952 | bytes 20000000 | tf_op jit(solution)/shard_map/factor/pallas_call | solution.py:181
  179.7 1.2 collective-permute-start
  180.9 0.6 pad_add_fusion.pick
  181.5 1.4 dynamic-slice_subtract_fusion.2
  183.0 15.1 %assemble.2.base_ref = f32[256,4096]{1,0:T(8,128)} custom-call(s32[2]{0:T(128)} %pad_add_fusion.1.pick, bf16[192,1536]{1,0:T(8,128)(2,1)} %get-tuple-element.8.g_ref, bf16[6144,1536]{1,0:T(8,128)(2,1)} %all-gather.4.cloned.1.call-done.b_ref, f32[192,6144]{1,0:T(8,128)} %bitcast.19, ...), custom_call_target="tpu_custom_call", output_to_operand_aliasing={{}: (6, {})} | custom-call | flops 5000000000 | bytes 20000000 | tf_op jit(solution)/shard_map/assemble/pallas_call | solution.py:222
  198.1 1.0 copy-done.1
  199.1 0.2 copy-done.2
  199.2 14.9 %assemble.3 = f32[256,4096]{1,0:T(8,128)} custom-call(s32[2]{0:T(128)} %pad_add_fusion.pick, bf16[192,1536]{1,0:T(8,128)(2,1)} %copy-done.2, bf16[6144,1536]{1,0:T(8,128)(2,1)} %all-gather.4.cloned.1.call-done.b_ref, bf16[192,3072]{1,0:T(8,128)(2,1)} %copy-done.1, s32[1,192]{1,0:T(1,128)} %get-tuple-element.12.rows_ref, ...), custom_call_target="tpu_custom_call", output_to_operand_aliasing={{}: (6, {})} | custom-call | flops 5000000000 | bytes 20000000 | tf_op jit(solution)/shard_map/assemble/pallas_call | solution.py:222
  (7 shorter events, 0.0 us)
Async XLA Ops:
  7.2 4.9 %copy-start = (f32[1,192,1536]{2,1,0:T(8,128)S(1)}, f32[1,192,1536]{2,1,0:T(8,128)}, u32[]{:S(2)}) copy-start(f32[1,192,1536]{2,1,0:T(8,128)} %param.6) | copy-start | bytes 3538948
  7.2 69.2 %all-gather.6.cloned.1.call-start = ((), (), s32[]{:S(2)}) async-start(), calls=%async_computation.1 | async-start | bytes 9732096 | tf_op jit(solution)/shard_map/all_gather | solution.py:266
  12.0 171.0 %all-gather.4.cloned.1.call-start = ((), (), s32[]{:S(2)}) async-start(), calls=%async_computation | async-start | bytes 19464192 | tf_op jit(solution)/shard_map/all_gather | solution.py:278
  12.1 0.7 collective-permute-start.1
  15.6 182.4 %collective-permute-start.2 = (bf16[192,3072]{1,0:T(8,128)(2,1)S(1)}, bf16[192,3072]{1,0:T(8,128)(2,1)S(1)}, u32[]{:S(2)}, u32[]{:S(2)}) collective-permute-start(bf16[192,3072]{1,0:T(8,128)(2,1)S(1)} %fusion), channel_id=1, source_target_pairs={{0,32},{1,33},{2,34},{3,35},{4,36},{5,37},{6,38},{7,39},{8,40},{9,... | collective-permute-start | bytes 3538952 | tf_op jit(solution)/shard_map/ppermute | solution.py:280
  179.7 18.4 %collective-permute-start = (bf16[192,1536]{1,0:T(8,128)(2,1)}, bf16[192,1536]{1,0:T(8,128)(2,1)S(1)}, u32[]{:S(2)}, u32[]{:S(2)}) collective-permute-start(bf16[192,1536]{1,0:T(8,128)(2,1)} %get-tuple-element.8.g_ref), channel_id=1, source_target_pairs={{0,32},{1,33},{2,34},{3,35},{4,36},{5,37},{6,38},{7,39},{8,40},{9,... | collective-permute-start | bytes 1769480 | tf_op jit(solution)/shard_map/ppermute | solution.py:284
  198.0 1.0 copy-start.1
  198.1 1.2 copy-start.2
Sparse Core Ops, SparseCore 0:
  12.1 64.2 all-gather.5
  78.6 77.0 all-gather.3

commit v2 on v1

--- a/solution.py
+++ b/solution.py
@@ -45,24 +45,49 @@
     return nn(left3(a), right3(b, 0))
 
 
-def factor_corner(work, segments=4):
+def factor_corner(work, keep, segments=2):
     count = DB // 8
     sub = lax.broadcasted_iota(jnp.int32, (8, DB), 0)
 
+    def wide(row):
+        return jnp.broadcast_to(row, (8, DB))
+
     def step(first, block, carry):
         start = pl.multiple_of(block * 8, 8)
-        rows_d = work[pl.ds(start, 8), :DB]
-        rows_e = work[pl.ds(start, 8), DB:]
+        after = pl.multiple_of(start + 8, 8)
+        before = pl.multiple_of(jnp.maximum(start - 8, 0), 8)
+        started = jnp.where(block > 0, 1.0, 0.0).astype(f32)
+        halves = (slice(0, DB), slice(DB, 2 * DB))
+        rows = [work[pl.ds(start, 8), h] for h in halves]
+        tile = [work[pl.ds(after, 8), h] for h in halves]
+        past = [keep[pl.ds(before, 8), h] for h in halves]
         lane = jnp.zeros((8, DB), jnp.int32) + start
-
-        def column(rows, k):
-            return jnp.take_along_axis(rows, lane + k, axis=1)
+        lane_before = jnp.zeros((8, DB), jnp.int32) + before
+
+        low = (first + 1) * 8
+        if low < DB:
+            left = work[low:DB, :DB]
+            place = lax.broadcasted_iota(jnp.int32, left.shape, 1)
+            depth = lax.broadcasted_iota(jnp.int32, left.shape, 0) + low
+            chosen = (place >= start - 8) & (place < start) & (depth >= start + 16)
+            left = jnp.where(chosen, left, 0.0)
+            change = nn3(left, keep[...])
+
+        for k in range(8):
+            coef = jnp.take_along_axis(tile[0], lane_before + k, axis=1) * started
+            if k == 0:
+                drop = [coef * wide(past[s][k:k + 1]) for s in range(2)]
+            else:
+                drop = [drop[s] + coef * wide(past[s][k:k + 1]) for s in range(2)]
+        tile = [tile[s] - drop[s] for s in range(2)]
 
         a = {}
+        side_col = []
         for k in range(8):
-            piece = column(rows_d, k)
+            piece = jnp.take_along_axis(rows[0], lane + k, axis=1)
             for s in range(k, 8):
-                a[s, k] = jnp.broadcast_to(piece[s:s + 1], (8, DB))
+                a[s, k] = wide(piece[s:s + 1])
+            side_col.append(jnp.take_along_axis(tile[0], lane + k, axis=1))
         r = []
         up = []
         for i in range(8):
@@ -73,42 +98,41 @@
             for k in range(i + 1, 8):
                 for j in range(i + 1, k + 1):
                     a[k, j] = a[k, j] - a[k, i] * a[j, i]
+            side_col[i] = side_col[i] * inv
+            for k in range(i + 1, 8):
+                side_col[k] = side_col[k] - a[k, i] * side_col[i]
+            if i == 0:
+                run = [[wide(rows[s][k:k + 1]) for k in range(8)] for s in range(2)]
             pair = []
-            for side, rows in enumerate((rows_d, rows_e)):
-                value = jnp.broadcast_to(rows[i:i + 1], (8, DB))
-                for k in range(i):
-                    value = value - a[i, k] * up[k][side]
-                pair.append(value * inv)
+            for s in range(2):
+                value = run[s][i] * inv
+                pair.append(value)
+                for k in range(i + 1, 8):
+                    run[s][k] = run[s][k] - a[k, i] * value
+                tile[s] = tile[s] - side_col[i] * value
             up.append(pair)
+        if low < DB:
+            work[low:DB, :] = work[low:DB, :] - change
+        for s in range(2):
+            work[pl.ds(after, 8), halves[s]] = tile[s]
+            value = up[0][s]
+            for i in range(1, 8):
+                value = jnp.where(sub == i, up[i][s], value)
+            work[pl.ds(start, 8), halves[s]] = value
         back = [None] * 8
         for i in reversed(range(8)):
             pair = []
-            for side in range(2):
-                value = up[i][side]
+            for s in range(2):
+                value = up[i][s]
                 for k in range(i + 1, 8):
-                    value = value - a[k, i] * back[k][side]
+                    value = value - a[k, i] * back[k][s]
                 pair.append(value * r[i])
             back[i] = pair
-        for side in range(2):
-            value = up[0][side]
+        for s in range(2):
+            value = back[0][s]
             for i in range(1, 8):
-                value = jnp.where(sub == i, up[i][side], value)
-            work[pl.ds(start, 8), side * DB:(side + 1) * DB] = value
-        for v in range(first + 1, count):
-            tile_d = work[v * 8:v * 8 + 8, :DB]
-            tile_e = work[v * 8:v * 8 + 8, DB:]
-            live = jnp.where(v > block, 1.0, 0.0).astype(f32)
-            sum_d = sum_e = None
-            for k in range(8):
-                coef = column(tile_d, k)
-                if k == 0:
-                    sum_d = coef * back[k][0]
-                    sum_e = coef * back[k][1]
-                else:
-                    sum_d = sum_d + coef * back[k][0]
-                    sum_e = sum_e + coef * back[k][1]
-            work[v * 8:v * 8 + 8, :DB] = tile_d - live * sum_d
-            work[v * 8:v * 8 + 8, DB:] = tile_e - live * sum_e
+                value = jnp.where(sub == i, back[i][s], value)
+            keep[pl.ds(start, 8), halves[s]] = value
         return carry
 
     size = count // segments
@@ -116,28 +140,32 @@
         lax.fori_loop(seg * size, (seg + 1) * size, lambda b, c, f=seg * size: step(f, b, c), 0)
 
 
-def factor_kernel(order, rows, where_ref, a_ref, b_ref, l_ref, x_ref, g_ref, m, work, inv, p_hi, p_lo):
+def factor_kernel(order, rows, where_ref, a_ref, b_ref, l_ref, x_ref, g_ref, m, work, keep, inv, p_hi, p_lo, fetch_sem):
     total = order + rows
     eye = (lax.broadcasted_iota(jnp.int32, (DB, DB), 0) == lax.broadcasted_iota(jnp.int32, (DB, DB), 1)).astype(f32)
     low_mask = lax.broadcasted_iota(jnp.int32, (DB, DB), 0) >= lax.broadcasted_iota(jnp.int32, (DB, DB), 1)
-    m[:order, :] = a_ref[...]
+    fetch = pltpu.make_async_copy(a_ref, m.at[:order, :], fetch_sem)
+    fetch.start()
     m[order:, :] = b_ref[...]
     zero = jnp.zeros((DB, DB), f32)
+    keep[...] = jnp.zeros_like(keep)
+    work[DB:, :] = jnp.zeros((8, 2 * DB), f32)
+    fetch.wait()
     for p in range(order // PB):
         c0 = p * PB
         c1 = c0 + DB
         c2 = c0 + PB
-        work[:, :DB] = m[c0:c1, c0:c1]
-        work[:, DB:] = eye
-        factor_corner(work)
-        l11 = jnp.where(low_mask, work[:, :DB].T, 0.0)
-        i11 = work[:, DB:]
+        work[:DB, :DB] = m[c0:c1, c0:c1]
+        work[:DB, DB:] = eye
+        factor_corner(work, keep)
+        l11 = jnp.where(low_mask, work[:DB, :DB].T, 0.0)
+        i11 = work[:DB, DB:]
         l21 = nt3(m[c1:c2, c0:c1], i11)
-        work[:, :DB] = m[c1:c2, c1:c2] - nt3(l21, l21)
-        work[:, DB:] = eye
-        factor_corner(work)
-        l22 = jnp.where(low_mask, work[:, :DB].T, 0.0)
-        i22 = work[:, DB:]
+        work[:DB, :DB] = m[c1:c2, c1:c2] - nt3(l21, l21)
+        work[:DB, DB:] = eye
+        factor_corner(work, keep)
+        l22 = jnp.where(low_mask, work[:DB, :DB].T, 0.0)
+        i22 = work[:DB, DB:]
         i21 = -nn3(i22, nn3(l21, i11))
         m[c0:c1, c0:c1] = l11
         m[c0:c1, c1:c2] = zero
@@ -174,6 +202,151 @@
         g_ref[:, c0:c2] = g.astype(bf16)
 
 
+MESH = pl.DeviceIdType.MESH
+
+
+def gather_kernel(own_ref, out_ref, send, local_sem, recv_f, recv_s, recv_c):
+    rows = own_ref.shape[0]
+    part = rows // 2
+    leaf = lax.axis_index("leaf")
+    z = lax.axis_index("prow")
+    pcol = lax.axis_index("pcol")
+    size = 4
+    x = pcol // 2
+    core = pcol % 2
+    flip = core == 1
+    f = jnp.where(flip, z, x)
+    s = jnp.where(flip, x, z)
+
+    def device(fi, si, ci):
+        zi = jnp.where(flip, fi, si)
+        xi = jnp.where(flip, si, fi)
+        return (leaf, zi, xi * 2 + ci)
+
+    def first(fi, si):
+        zi = jnp.where(flip, fi, si)
+        xi = jnp.where(flip, si, fi)
+        return (zi * 2 * size + xi * 2 + core) * rows
+
+    def window(fi, si, piece):
+        top = first(fi, si)
+        if piece is None:
+            return out_ref.at[pl.ds(pl.multiple_of(top, 8), rows), :]
+        return out_ref.at[pl.ds(pl.multiple_of(top + piece * part, 8), part), :]
+
+    def near(v, d):
+        return (v + d + size) % size
+
+    f_dev = [device(near(f, 1), s, core), device(near(f, -1), s, core)]
+    s_dev = [device(f, near(s, 1), core), device(f, near(s, -1), core)]
+    twin = device(f, s, 1 - core)
+
+    barrier = pltpu.get_barrier_semaphore()
+    for dev in f_dev + s_dev + [twin]:
+        pl.semaphore_signal(barrier, inc=1, device_id=dev, device_id_type=MESH)
+    pl.semaphore_wait(barrier, 5)
+
+    started = []
+
+    def push(src, dst, recv_sem, dev):
+        copy = pltpu.make_async_remote_copy(
+            src_ref=src, dst_ref=dst, send_sem=send.at[len(started)], recv_sem=recv_sem,
+            device_id=dev, device_id_type=MESH,
+        )
+        copy.start()
+        started.append(copy)
+
+    def arrived(dst, recv_sem):
+        pltpu.make_async_remote_copy(
+            src_ref=dst, dst_ref=dst, send_sem=send.at[0], recv_sem=recv_sem,
+            device_id=twin, device_id_type=MESH,
+        ).wait_recv()
+
+    offsets = [0, -1, 1, 2]
+
+    def pass_on(k, src, fi):
+        dst = window(fi, s, None)
+        for d in range(2):
+            push(src, dst, recv_s.at[k, d], s_dev[d])
+        push(src, dst, recv_c.at[0, k], twin)
+
+    own_dst = window(f, s, None)
+    for d in range(2):
+        push(own_ref, own_dst, recv_f.at[d], f_dev[d])
+    pass_on(0, own_ref, f)
+    keep = pltpu.make_async_copy(own_ref, own_dst, local_sem)
+    keep.start()
+
+    for d, off in ((0, -1), (1, 1)):
+        fi = near(f, off)
+        arrived(window(fi, s, None), recv_f.at[d])
+        push(window(fi, s, d), window(fi, s, d), recv_f.at[2 + d], f_dev[d])
+        pass_on(1 + d, window(fi, s, None), fi)
+
+    def second(k):
+        fi = near(f, offsets[k])
+        for d, off in ((0, -1), (1, 1)):
+            si = near(s, off)
+            arrived(window(fi, si, None), recv_s.at[k, d])
+            push(window(fi, si, d), window(fi, si, d), recv_s.at[k, 2 + d], s_dev[d])
+            push(window(fi, si, None), window(fi, si, None), recv_c.at[1 + d, k], twin)
+
+    def third(k):
+        fi = near(f, offsets[k])
+        si = near(s, 2)
+        for d in range(2):
+            arrived(window(fi, si, d), recv_s.at[k, 2 + d])
+        push(window(fi, si, None), window(fi, si, None), recv_c.at[3, k], twin)
+
+    second(0)
+    fi = near(f, 2)
+    for d in range(2):
+        arrived(window(fi, s, d), recv_f.at[2 + d])
+    pass_on(3, window(fi, s, None), fi)
+    second(1)
+    third(0)
+    second(2)
+    third(1)
+    second(3)
+    third(2)
+    third(3)
+
+    def twin_window(a, b):
+        tf, ts = s, f
+        fi = near(tf, offsets[b])
+        si = near(ts, (0, -1, 1, 2)[a])
+        zi = jnp.where(flip, si, fi)
+        xi = jnp.where(flip, fi, si)
+        top = (zi * 2 * size + xi * 2 + (1 - core)) * rows
+        return out_ref.at[pl.ds(pl.multiple_of(top, 8), rows), :]
+
+    for a in range(4):
+        for b in range(4):
+            arrived(twin_window(a, b), recv_c.at[a, b])
+    for copy in started:
+        copy.wait_send()
+    keep.wait()
+
+
+def gather_rows(own, count):
+    any_spec = pl.BlockSpec(memory_space=pl.ANY)
+    return pl.pallas_call(
+        gather_kernel,
+        out_shape=jax.ShapeDtypeStruct((own.shape[0] * count, own.shape[1]), own.dtype),
+        in_specs=[any_spec],
+        out_specs=any_spec,
+        scratch_shapes=[
+            pltpu.SemaphoreType.DMA((40,)),
+            pltpu.SemaphoreType.DMA,
+            pltpu.SemaphoreType.DMA((4,)),
+            pltpu.SemaphoreType.DMA((4, 4)),
+            pltpu.SemaphoreType.DMA((4, 4)),
+        ],
+        compiler_params=pltpu.CompilerParams(collective_id=0, has_side_effects=True),
+        name="gather_rows",
+    )(own)
+
+
 def factor(where, a, b, held):
     order = a.shape[0]
     rows = b.shape[0]
@@ -185,17 +358,19 @@
             jax.ShapeDtypeStruct((rows, order), f32),
             jax.ShapeDtypeStruct((rows, order), bf16),
         ),
-        in_specs=[pl.BlockSpec(memory_space=pltpu.SMEM), vm, vm],
+        in_specs=[pl.BlockSpec(memory_space=pltpu.SMEM), pl.BlockSpec(memory_space=pl.ANY), vm],
         out_specs=(vm, vm, vm),
         scratch_shapes=[
             pltpu.VMEM((order + rows, order), f32),
+            pltpu.VMEM((DB + 8, 2 * DB), f32),
             pltpu.VMEM((DB, 2 * DB), f32),
             pltpu.VMEM((order, PB), f32),
             pltpu.VMEM((order + rows, PB), bf16),
             pltpu.VMEM((order + rows, PB), bf16),
+            pltpu.SemaphoreType.DMA,
         ],
         compiler_params=pltpu.CompilerParams(vmem_limit_bytes=60 * 2**20),
-        cost_estimate=pl.CostEstimate(flops=100 * 10**9, bytes_accessed=2 * 10**7, transcendentals=0),
+        cost_estimate=pl.CostEstimate(flops=70 * 10**9, bytes_accessed=2 * 10**7, transcendentals=0),
         name="factor",
     )(where, a, b)
 
@@ -263,7 +438,7 @@
     wide = half // steps
     window = parent_half // steps
 
-    matrix = lax.all_gather(pivot_rows, ("prow", "pcol"), axis=0, tiled=True)
+    matrix = gather_rows(pivot_rows, spots)
 
     low_bits = lower_rows.astype(bf16)
     swap = []
@@ -274,9 +449,11 @@
             if spot // half_spots != one % 2:
                 swap.append((one * spots + spot, (one ^ 1) * spots + (spot ^ half_spots)))
     swapped = lax.ppermute(low_bits, AXES, swap)
+    swapped, matrix = lax.optimization_barrier((swapped, matrix))
     block = jnp.where(position // half_spots == side, low_bits, swapped)
     b_all = lax.all_gather(block, ("prow", "pcol"), axis=0, tiled=True)
     other = lax.dynamic_slice_in_dim(rest_rows, (1 - side) * half, half, 1).astype(bf16)
+    other, matrix = lax.optimization_barrier((other, matrix))
     rest_sib = lax.ppermute(other, AXES, mirror)
 
     where = jnp.full((1,), position, jnp.int32)

time: 222 us -> 181 us (0.82)
  waiting for transfers between devices: 38.6 us -> 1.09 us
  starting transfers between devices: 21.9 us -> 2.36 us
  Pallas kernels: 133 us -> 149 us
    pallas_call x0 -> x1, Pallas kernels: none -> 50.5 us  [gather_rows(): pl.pallas_call(gather_kernel, out_shape=jax.ShapeDtypeStruct((own.shape[0...]
    all_gather x1 -> x0, waiting for transfers between devices: 38.5 us -> none  [local(): matrix = lax.all_gather(pivot_rows, ('prow', 'pcol'), axis=0, tiled=True)]
    pallas_call x1, Pallas kernels: 103 us -> 68.4 us  [factor(): pl.pallas_call(functools.partial(factor_kernel, order, rows), out_shape=(...]
    ppermute x1, starting transfers between devices: 20 us -> 0.09 us  [local(): rest_sib = lax.ppermute(other, AXES, mirror)]
  transfers between devices with their start and end apart: 5 -> 4, of which waited for: 1 -> 1; matrix products, arithmetic and copies ran while one was open for 3% -> 3% of each run, Pallas kernels for 54% -> 75%
where the time goes in v2:
time: 181 us; the launch traced here: 180 us
  Pallas kernels  149 us (82%)
  between operations  14.2 us (8%)
  local copies, waits for them, and re-layouts  7.76 us (4%)
  other arithmetic  5.35 us (3%)
  starting transfers between devices  2.36 us (1%)
    pallas_call x1, Pallas kernels, factor(): pl.pallas_call(functools.partial(factor_kernel, order, rows), out_shape=(...  68.4 us
    pallas_call x1, Pallas kernels, gather_rows(): pl.pallas_call(gather_kernel, out_shape=jax.ShapeDtypeStruct((own.shape[0...  50.5 us
    pallas_call x2, Pallas kernels, assemble(): pl.pallas_call(assemble_kernel, out_shape=jax.ShapeDtypeStruct(base.shape...  30 us
    unnamed x7, local copies, waits for them, and re-layouts  5.94 us
  transfers between devices with their start and end apart: 4, of which 1 were waited for; matrix products, arithmetic and copies ran while one was open for 3% of the time, Pallas kernels for 75%

profile of v2, /device:TPU:1, one launch (start us, length us, event | category | flops | bytes accessed | tf_op | source)
XLA Modules:
  0.0 179.7 jit_solution(10191158679436690430)
XLA Ops:
  7.2 0.0 copy-start
  7.2 0.0 all-gather.2.cloned.1.call-start
  7.2 4.7 %copy.13 = f32[1,256,4096]{2,1,0:T(8,128)} copy(f32[1,256,4096]{2,1,0:T(8,128)} %param.8) | data formatting | bytes 8388608
  12.0 0.1 bitcast_convert_fusion
  12.0 0.7 collective-permute-start
  12.8 50.5 %gather_rows.1.a_ref = f32[1536,1536]{1,0:T(8,128)} custom-call(f32[48,1536]{1,0:T(8,128)} %bitcast.21), custom_call_target="tpu_custom_call" | custom-call | tf_op jit(solution)/shard_map/gather_rows/pallas_call | solution.py:333
  63.3 0.0 collective-permute-done
  63.3 0.9 broadcast_select_fusion
  64.2 0.0 all-gather.2.cloned.1.call-update
  64.3 0.6 pad_add_fusion.1.pick
  64.9 1.0 dynamic-slice_subtract_fusion
  65.9 0.7 broadcast_subtract_fusion
  66.6 1.8 %fusion = bf16[192,3072]{1,0:T(8,128)(2,1)S(1)} fusion(f32[1,192,6144]{2,1,0:T(8,128)} %param.7, s32[]{:T(128)S(6)} %select_n.46), kind=kLoop, calls=%fused_computation.1 | loop fusion | bytes 2359300 | tf_op jit(solution)/shard_map/convert_element_type | solution.py:455
  68.4 0.1 collective-permute-start.2
  68.5 68.4 %factor.1 = (f32[48,1536]{1,0:T(8,128)}, f32[192,1536]{1,0:T(8,128)}, bf16[192,1536]{1,0:T(8,128)(2,1)}) custom-call(s32[1]{0:T(128)} %bitcast.where_ref, f32[1536,1536]{1,0:T(8,128)} %gather_rows.1.a_ref, f32[192,1536]{1,0:T(8,128)} %bitcast.20), custom_call_target="tpu_custom_call" | custom-call | flops 70000001024 | bytes 20000000 | tf_op jit(solution)/shard_map/factor/pallas_call | solution.py:354
  137.0 1.5 collective-permute-start.1
  138.5 0.6 pad_add_fusion.pick
  139.1 1.4 dynamic-slice_subtract_fusion.2
  140.6 1.1 all-gather.2.cloned.1.call-done.b_ref
  141.6 15.1 %assemble.2.base_ref = f32[256,4096]{1,0:T(8,128)} custom-call(s32[2]{0:T(128)} %pad_add_fusion.1.pick, bf16[192,1536]{1,0:T(8,128)(2,1)} %get-tuple-element.14.g_ref, bf16[6144,1536]{1,0:T(8,128)(2,1)} %all-gather.2.cloned.1.call-done.b_ref, f32[192,6144]{1,0:T(8,128)} %bitcast.19, ...), custom_call_target="tpu_custom_call", output_to_operand_aliasing={{}: (6, {})} | custom-call | flops 5000000000 | bytes 20000000 | tf_op jit(solution)/shard_map/assemble/pallas_call | solution.py:397
  156.7 0.0 collective-permute-done.1.g_ref
  156.7 0.8 copy-done.2
  157.5 0.4 copy-done.1
  157.9 14.9 %assemble.3 = f32[256,4096]{1,0:T(8,128)} custom-call(s32[2]{0:T(128)} %pad_add_fusion.pick, bf16[192,1536]{1,0:T(8,128)(2,1)} %copy-done.2, bf16[6144,1536]{1,0:T(8,128)(2,1)} %all-gather.2.cloned.1.call-done.b_ref, bf16[192,3072]{1,0:T(8,128)(2,1)} %copy-done.1, s32[1,192]{1,0:T(1,128)} %get-tuple-element.20.rows_ref, ...), custom_call_target="tpu_custom_call", output_to_operand_aliasing={{}: (6, {})} | custom-call | flops 5000000000 | bytes 20000000 | tf_op jit(solution)/shard_map/assemble/pallas_call | solution.py:397
  (5 shorter events, 0.0 us)
Async XLA Ops:
  7.2 4.8 %copy-start = (f32[1,192,1536]{2,1,0:T(8,128)S(1)}, f32[1,192,1536]{2,1,0:T(8,128)}, u32[]{:S(2)}) copy-start(f32[1,192,1536]{2,1,0:T(8,128)} %param.6) | copy-start | bytes 3538948
  7.2 134.5 %all-gather.2.cloned.1.call-start = ((), (), s32[]{:S(2)}) async-start(), calls=%async_computation | async-start | bytes 19464192 | tf_op jit(solution)/shard_map/all_gather | solution.py:454
  12.0 51.3 %collective-permute-start = (bf16[192,1536]{1,0:T(8,128)(2,1)S(1)}, bf16[192,1536]{1,0:T(8,128)(2,1)S(1)}, u32[]{:S(2)}, u32[]{:S(2)}) collective-permute-start(bf16[192,1536]{1,0:T(8,128)(2,1)S(1)} %bitcast_convert_fusion), channel_id=1, source_target_pairs={{16,32},{17,33},{18,34},{19,35},{20,36},{21,37},{22,38},{23,39},{2... | collective-permute-start | bytes 1769480 | tf_op jit(solution)/shard_map/ppermute | solution.py:451
  68.4 88.3 %collective-permute-start.2 = (bf16[192,3072]{1,0:T(8,128)(2,1)S(1)}, bf16[192,3072]{1,0:T(8,128)(2,1)S(1)}, u32[]{:S(2)}, u32[]{:S(2)}) collective-permute-start(bf16[192,3072]{1,0:T(8,128)(2,1)S(1)} %fusion), channel_id=1, source_target_pairs={{0,32},{1,33},{2,34},{3,35},{4,36},{5,37},{6,38},{7,39},{8,40},{9,... | collective-permute-start | bytes 3538952 | tf_op jit(solution)/shard_map/ppermute | solution.py:457
  137.0 19.7 %collective-permute-start.1 = (bf16[192,1536]{1,0:T(8,128)(2,1)}, bf16[192,1536]{1,0:T(8,128)(2,1)S(1)}, u32[]{:S(2)}, u32[]{:S(2)}) collective-permute-start(bf16[192,1536]{1,0:T(8,128)(2,1)} %get-tuple-element.14.g_ref), channel_id=1, source_target_pairs={{0,32},{1,33},{2,34},{3,35},{4,36},{5,37},{6,38},{7,39},{8,40},{9,... | collective-permute-start | bytes 1769480 | tf_op jit(solution)/shard_map/ppermute | solution.py:461
  156.7 0.8 copy-start.2
  156.7 1.2 copy-start.1
Sparse Core Ops, SparseCore 0:
  64.4 77.2 all-gather.1

commit v3 on v2

--- a/solution.py
+++ b/solution.py
@@ -140,17 +140,141 @@
         lax.fori_loop(seg * size, (seg + 1) * size, lambda b, c, f=seg * size: step(f, b, c), 0)
 
 
-def factor_kernel(order, rows, where_ref, a_ref, b_ref, l_ref, x_ref, g_ref, m, work, keep, inv, p_hi, p_lo, fetch_sem):
+MESH = pl.DeviceIdType.MESH
+
+
+def gather_pivots(own_ref, out_ref, send, local_sem, recv_f, recv_s, recv_c):
+    rows = own_ref.shape[0]
+    part = rows // 2
+    leaf = lax.axis_index("leaf")
+    z = lax.axis_index("prow")
+    pcol = lax.axis_index("pcol")
+    size = 4
+    x = pcol // 2
+    core = pcol % 2
+    flip = core == 1
+    f = jnp.where(flip, z, x)
+    s = jnp.where(flip, x, z)
+
+    def device(fi, si, ci):
+        zi = jnp.where(flip, fi, si)
+        xi = jnp.where(flip, si, fi)
+        return (leaf, zi, xi * 2 + ci)
+
+    def first(fi, si):
+        zi = jnp.where(flip, fi, si)
+        xi = jnp.where(flip, si, fi)
+        return (zi * 2 * size + xi * 2 + core) * rows
+
+    def window(fi, si, piece):
+        top = first(fi, si)
+        if piece is None:
+            return out_ref.at[pl.ds(pl.multiple_of(top, 8), rows), :]
+        return out_ref.at[pl.ds(pl.multiple_of(top + piece * part, 8), part), :]
+
+    def near(v, d):
+        return (v + d + size) % size
+
+    f_dev = [device(near(f, 1), s, core), device(near(f, -1), s, core)]
+    s_dev = [device(f, near(s, 1), core), device(f, near(s, -1), core)]
+    twin = device(f, s, 1 - core)
+
+    barrier = pltpu.get_barrier_semaphore()
+    for dev in f_dev + s_dev + [twin]:
+        pl.semaphore_signal(barrier, inc=1, device_id=dev, device_id_type=MESH)
+    pl.semaphore_wait(barrier, 5)
+
+    started = []
+
+    def push(src, dst, recv_sem, dev):
+        copy = pltpu.make_async_remote_copy(
+            src_ref=src, dst_ref=dst, send_sem=send.at[len(started)], recv_sem=recv_sem,
+            device_id=dev, device_id_type=MESH,
+        )
+        copy.start()
+        started.append(copy)
+
+    def arrived(dst, recv_sem):
+        pltpu.make_async_remote_copy(
+            src_ref=dst, dst_ref=dst, send_sem=send.at[0], recv_sem=recv_sem,
+            device_id=twin, device_id_type=MESH,
+        ).wait_recv()
+
+    offsets = [0, -1, 1, 2]
+
+    def pass_on(k, src, fi):
+        dst = window(fi, s, None)
+        for d in range(2):
+            push(src, dst, recv_s.at[k, d], s_dev[d])
+        push(src, dst, recv_c.at[0, k], twin)
+
+    own_dst = window(f, s, None)
+    for d in range(2):
+        push(own_ref, own_dst, recv_f.at[d], f_dev[d])
+    pass_on(0, own_ref, f)
+    keep = pltpu.make_async_copy(own_ref, own_dst, local_sem)
+    keep.start()
+
+    for d, off in ((0, -1), (1, 1)):
+        fi = near(f, off)
+        arrived(window(fi, s, None), recv_f.at[d])
+        push(window(fi, s, d), window(fi, s, d), recv_f.at[2 + d], f_dev[d])
+        pass_on(1 + d, window(fi, s, None), fi)
+
+    def second(k):
+        fi = near(f, offsets[k])
+        for d, off in ((0, -1), (1, 1)):
+            si = near(s, off)
+            arrived(window(fi, si, None), recv_s.at[k, d])
+            push(window(fi, si, d), window(fi, si, d), recv_s.at[k, 2 + d], s_dev[d])
+            push(window(fi, si, None), window(fi, si, None), recv_c.at[1 + d, k], twin)
+
+    def third(k):
+        fi = near(f, offsets[k])
+        si = near(s, 2)
+        for d in range(2):
+            arrived(window(fi, si, d), recv_s.at[k, 2 + d])
+        push(window(fi, si, None), window(fi, si, None), recv_c.at[3, k], twin)
+
+    second(0)
+    fi = near(f, 2)
+    for d in range(2):
+        arrived(window(fi, s, d), recv_f.at[2 + d])
+    pass_on(3, window(fi, s, None), fi)
+    second(1)
+    third(0)
+    second(2)
+    third(1)
+    second(3)
+    third(2)
+    third(3)
+
+    def twin_window(a, b):
+        tf, ts = s, f
+        fi = near(tf, offsets[b])
+        si = near(ts, (0, -1, 1, 2)[a])
+        zi = jnp.where(flip, si, fi)
+        xi = jnp.where(flip, fi, si)
+        top = (zi * 2 * size + xi * 2 + (1 - core)) * rows
+        return out_ref.at[pl.ds(pl.multiple_of(top, 8), rows), :]
+
+    for a in range(4):
+        for b in range(4):
+            arrived(twin_window(a, b), recv_c.at[a, b])
+    for copy in started:
+        copy.wait_send()
+    keep.wait()
+
+
+def factor_kernel(order, rows, a_ref, b_ref, l_ref, x_ref, g_ref, m, work, keep, inv, p_hi, p_lo, send, local_sem, recv_f, recv_s, recv_c):
     total = order + rows
     eye = (lax.broadcasted_iota(jnp.int32, (DB, DB), 0) == lax.broadcasted_iota(jnp.int32, (DB, DB), 1)).astype(f32)
     low_mask = lax.broadcasted_iota(jnp.int32, (DB, DB), 0) >= lax.broadcasted_iota(jnp.int32, (DB, DB), 1)
-    fetch = pltpu.make_async_copy(a_ref, m.at[:order, :], fetch_sem)
-    fetch.start()
     m[order:, :] = b_ref[...]
     zero = jnp.zeros((DB, DB), f32)
     keep[...] = jnp.zeros_like(keep)
     work[DB:, :] = jnp.zeros((8, 2 * DB), f32)
-    fetch.wait()
+    gather_pivots(a_ref, m, send, local_sem, recv_f, recv_s, recv_c)
     for p in range(order // PB):
         c0 = p * PB
         c1 = c0 + DB
@@ -186,7 +310,7 @@
             m[j:, j:j + PB] = m[j:, j:j + PB] - nt(left, right)
     x_ref[...] = m[order:, :]
     held = l_ref.shape[0]
-    top = pl.multiple_of(where_ref[0] * held, 8)
+    top = pl.multiple_of(lax.axis_index(("prow", "pcol")) * held, 8)
     own = m[pl.ds(top, held), :]
     row_id = lax.broadcasted_iota(jnp.int32, own.shape, 0) + top
     col_id = lax.broadcasted_iota(jnp.int32, own.shape, 1)
@@ -202,153 +326,8 @@
         g_ref[:, c0:c2] = g.astype(bf16)
 
 
-MESH = pl.DeviceIdType.MESH
-
-
-def gather_kernel(own_ref, out_ref, send, local_sem, recv_f, recv_s, recv_c):
-    rows = own_ref.shape[0]
-    part = rows // 2
-    leaf = lax.axis_index("leaf")
-    z = lax.axis_index("prow")
-    pcol = lax.axis_index("pcol")
-    size = 4
-    x = pcol // 2
-    core = pcol % 2
-    flip = core == 1
-    f = jnp.where(flip, z, x)
-    s = jnp.where(flip, x, z)
-
-    def device(fi, si, ci):
-        zi = jnp.where(flip, fi, si)
-        xi = jnp.where(flip, si, fi)
-        return (leaf, zi, xi * 2 + ci)
-
-    def first(fi, si):
-        zi = jnp.where(flip, fi, si)
-        xi = jnp.where(flip, si, fi)
-        return (zi * 2 * size + xi * 2 + core) * rows
-
-    def window(fi, si, piece):
-        top = first(fi, si)
-        if piece is None:
-            return out_ref.at[pl.ds(pl.multiple_of(top, 8), rows), :]
-        return out_ref.at[pl.ds(pl.multiple_of(top + piece * part, 8), part), :]
-
-    def near(v, d):
-        return (v + d + size) % size
-
-    f_dev = [device(near(f, 1), s, core), device(near(f, -1), s, core)]
-    s_dev = [device(f, near(s, 1), core), device(f, near(s, -1), core)]
-    twin = device(f, s, 1 - core)
-
-    barrier = pltpu.get_barrier_semaphore()
-    for dev in f_dev + s_dev + [twin]:
-        pl.semaphore_signal(barrier, inc=1, device_id=dev, device_id_type=MESH)
-    pl.semaphore_wait(barrier, 5)
-
-    started = []
-
-    def push(src, dst, recv_sem, dev):
-        copy = pltpu.make_async_remote_copy(
-            src_ref=src, dst_ref=dst, send_sem=send.at[len(started)], recv_sem=recv_sem,
-            device_id=dev, device_id_type=MESH,
-        )
-        copy.start()
-        started.append(copy)
-
-    def arrived(dst, recv_sem):
-        pltpu.make_async_remote_copy(
-            src_ref=dst, dst_ref=dst, send_sem=send.at[0], recv_sem=recv_sem,
-            device_id=twin, device_id_type=MESH,
-        ).wait_recv()
-
-    offsets = [0, -1, 1, 2]
-
-    def pass_on(k, src, fi):
-        dst = window(fi, s, None)
-        for d in range(2):
-            push(src, dst, recv_s.at[k, d], s_dev[d])
-        push(src, dst, recv_c.at[0, k], twin)
-
-    own_dst = window(f, s, None)
-    for d in range(2):
-        push(own_ref, own_dst, recv_f.at[d], f_dev[d])
-    pass_on(0, own_ref, f)
-    keep = pltpu.make_async_copy(own_ref, own_dst, local_sem)
-    keep.start()
-
-    for d, off in ((0, -1), (1, 1)):
-        fi = near(f, off)
-        arrived(window(fi, s, None), recv_f.at[d])
-        push(window(fi, s, d), window(fi, s, d), recv_f.at[2 + d], f_dev[d])
-        pass_on(1 + d, window(fi, s, None), fi)
-
-    def second(k):
-        fi = near(f, offsets[k])
-        for d, off in ((0, -1), (1, 1)):
-            si = near(s, off)
-            arrived(window(fi, si, None), recv_s.at[k, d])
-            push(window(fi, si, d), window(fi, si, d), recv_s.at[k, 2 + d], s_dev[d])
-            push(window(fi, si, None), window(fi, si, None), recv_c.at[1 + d, k], twin)
-
-    def third(k):
-        fi = near(f, offsets[k])
-        si = near(s, 2)
-        for d in range(2):
-            arrived(window(fi, si, d), recv_s.at[k, 2 + d])
-        push(window(fi, si, None), window(fi, si, None), recv_c.at[3, k], twin)
-
-    second(0)
-    fi = near(f, 2)
-    for d in range(2):
-        arrived(window(fi, s, d), recv_f.at[2 + d])
-    pass_on(3, window(fi, s, None), fi)
-    second(1)
-    third(0)
-    second(2)
-    third(1)
-    second(3)
-    third(2)
-    third(3)
-
-    def twin_window(a, b):
-        tf, ts = s, f
-        fi = near(tf, offsets[b])
-        si = near(ts, (0, -1, 1, 2)[a])
-        zi = jnp.where(flip, si, fi)
-        xi = jnp.where(flip, fi, si)
-        top = (zi * 2 * size + xi * 2 + (1 - core)) * rows
-        return out_ref.at[pl.ds(pl.multiple_of(top, 8), rows), :]
-
-    for a in range(4):
-        for b in range(4):
-            arrived(twin_window(a, b), recv_c.at[a, b])
-    for copy in started:
-        copy.wait_send()
-    keep.wait()
-
-
-def gather_rows(own, count):
-    any_spec = pl.BlockSpec(memory_space=pl.ANY)
-    return pl.pallas_call(
-        gather_kernel,
-        out_shape=jax.ShapeDtypeStruct((own.shape[0] * count, own.shape[1]), own.dtype),
-        in_specs=[any_spec],
-        out_specs=any_spec,
-        scratch_shapes=[
-            pltpu.SemaphoreType.DMA((40,)),
-            pltpu.SemaphoreType.DMA,
-            pltpu.SemaphoreType.DMA((4,)),
-            pltpu.SemaphoreType.DMA((4, 4)),
-            pltpu.SemaphoreType.DMA((4, 4)),
-        ],
-        compiler_params=pltpu.CompilerParams(collective_id=0, has_side_effects=True),
-        name="gather_rows",
-    )(own)
-
-
-def factor(where, a, b, held):
-    order = a.shape[0]
+def factor(a, b, held):
+    order = a.shape[1]
     rows = b.shape[0]
     vm = pl.BlockSpec(memory_space=pltpu.VMEM)
     return pl.pallas_call(
@@ -358,7 +337,7 @@
             jax.ShapeDtypeStruct((rows, order), f32),
             jax.ShapeDtypeStruct((rows, order), bf16),
         ),
-        in_specs=[pl.BlockSpec(memory_space=pltpu.SMEM), pl.BlockSpec(memory_space=pl.ANY), vm],
+        in_specs=[pl.BlockSpec(memory_space=pl.ANY), vm],
         out_specs=(vm, vm, vm),
         scratch_shapes=[
             pltpu.VMEM((order + rows, order), f32),
@@ -367,12 +346,18 @@
             pltpu.VMEM((order, PB), f32),
             pltpu.VMEM((order + rows, PB), bf16),
             pltpu.VMEM((order + rows, PB), bf16),
+            pltpu.SemaphoreType.DMA((40,)),
             pltpu.SemaphoreType.DMA,
+            pltpu.SemaphoreType.DMA((4,)),
+            pltpu.SemaphoreType.DMA((4, 4)),
+            pltpu.SemaphoreType.DMA((4, 4)),
         ],
-        compiler_params=pltpu.CompilerParams(vmem_limit_bytes=60 * 2**20),
+        compiler_params=pltpu.CompilerParams(
+            vmem_limit_bytes=60 * 2**20, collective_id=0, has_side_effects=True
+        ),
         cost_estimate=pl.CostEstimate(flops=70 * 10**9, bytes_accessed=2 * 10**7, transcendentals=0),
         name="factor",
-    )(where, a, b)
+    )(a, b)
 
 
 def assemble_kernel(pick, g_ref, b_ref, c_ref, rows_ref, cols_ref, base_ref, out_ref):
@@ -389,7 +374,7 @@
     out_ref[...] = base_ref[...] + (nn(row_table, high) + nn(row_table, low))
 
 
-def assemble(pick, g, b_all, c, row_link, col_link, base):
+def assemble(pick, g, b_all, c, row_link, col_link, base, reuse):
     steps, _, wide = col_link.shape
     rows, order = g.shape
     height, full = base.shape
@@ -410,7 +395,7 @@
             ],
             out_specs=pl.BlockSpec((height, window), lambda t, pick: (0, t)),
         ),
-        input_output_aliases={6: 0},
+        input_output_aliases={6: 0} if reuse else {},
         cost_estimate=pl.CostEstimate(flops=5 * 10**9, bytes_accessed=2 * 10**7, transcendentals=0),
         name="assemble",
     )(pick, g, b_all, c, row_link, col_link, base)
@@ -438,7 +423,6 @@
     wide = half // steps
     window = parent_half // steps
 
-    matrix = gather_rows(pivot_rows, spots)
 
     low_bits = lower_rows.astype(bf16)
     swap = []
@@ -449,15 +433,12 @@
             if spot // half_spots != one % 2:
                 swap.append((one * spots + spot, (one ^ 1) * spots + (spot ^ half_spots)))
     swapped = lax.ppermute(low_bits, AXES, swap)
-    swapped, matrix = lax.optimization_barrier((swapped, matrix))
     block = jnp.where(position // half_spots == side, low_bits, swapped)
     b_all = lax.all_gather(block, ("prow", "pcol"), axis=0, tiled=True)
     other = lax.dynamic_slice_in_dim(rest_rows, (1 - side) * half, half, 1).astype(bf16)
-    other, matrix = lax.optimization_barrier((other, matrix))
     rest_sib = lax.ppermute(other, AXES, mirror)
 
-    where = jnp.full((1,), position, jnp.int32)
-    pivot_out, lower_out, g = factor(where, matrix, lower_rows, pivot_rows.shape[0])
+    pivot_out, lower_out, g = factor(pivot_rows, lower_rows, pivot_rows.shape[0])
     g_sib = lax.ppermute(g, AXES, mirror)
 
     def links(child):
@@ -471,8 +452,8 @@
     row_sib, col_sib = links(partner)
     pick_own = jnp.stack([side * steps, side * steps]).astype(jnp.int32)
     pick_sib = jnp.stack([(1 - side) * steps, 0 * side]).astype(jnp.int32)
-    merged = assemble(pick_own, g, b_all, rest_rows, row_own, col_own, base)
-    merged = assemble(pick_sib, g_sib, b_all, rest_sib, row_sib, col_sib, merged)
+    merged = assemble(pick_own, g, b_all, rest_rows, row_own, col_own, base, False)
+    merged = assemble(pick_sib, g_sib, b_all, rest_sib, row_sib, col_sib, merged, True)
     return (pivot_out[None], lower_out[None], merged[None])
 
 

time: 181 us -> 188 us (1.039)
  starting transfers between devices: 2.36 us -> 23.1 us
  Pallas kernels: 149 us -> 139 us
  local copies, waits for them, and re-layouts: 7.76 us -> 4.75 us
    pallas_call x1 -> x0, Pallas kernels: 50.5 us -> none  [gather_rows(): pl.pallas_call(gather_kernel, out_shape=jax.ShapeDtypeStruct((own.shape[0...]
    pallas_call x1, Pallas kernels: 68.4 us -> 109 us  [factor(): pl.pallas_call(functools.partial(factor_kernel, order, rows), out_shape=(...]
    ppermute x1, starting transfers between devices: 0.09 us -> 20 us  [local(): rest_sib = lax.ppermute(other, AXES, mirror)]
    unnamed x7 -> x12, local copies, waits for them, and re-layouts: 5.94 us -> 2.93 us
  transfers between devices with their start and end apart: 4 -> 4, of which waited for: 1 -> 0; matrix products, arithmetic and copies ran while one was open for 3% -> 3% of each run, Pallas kernels for 75% -> 66%
where the time goes in v3:
time: 188 us; the launch traced here: 187 us
  Pallas kernels  139 us (74%)
  starting transfers between devices  23.1 us (12%)
  between operations  14.2 us (8%)
  other arithmetic  6.67 us (4%)
  local copies, waits for them, and re-layouts  4.75 us (3%)
    pallas_call x1, Pallas kernels, factor(): pl.pallas_call(functools.partial(factor_kernel, order, rows), out_shape=(...  109 us
    pallas_call x2, Pallas kernels, assemble(): pl.pallas_call(assemble_kernel, out_shape=jax.ShapeDtypeStruct(base.shape...  30.2 us
    ppermute x1, starting transfers between devices, local(): rest_sib = lax.ppermute(other, AXES, mirror)  20 us
  transfers between devices with their start and end apart: 4, of which 0 were waited for; matrix products, arithmetic and copies ran while one was open for 3% of the time, Pallas kernels for 66%

profile of v3, /device:TPU:1, one launch (start us, length us, event | category | flops | bytes accessed | tf_op | source)
XLA Modules:
  0.0 187.4 jit_solution(7890377139023736355)
XLA Ops:
  7.2 0.0 copy-start
  7.2 0.0 all-gather.2.cloned.1.call-start
  7.2 1.4 bitcast_convert_fusion
  8.6 0.7 collective-permute-start.1
  9.4 0.0 collective-permute-done.1
  9.4 0.9 broadcast_select_fusion
  10.3 0.0 all-gather.2.cloned.1.call-update
  10.3 1.8 fusion
  12.2 20.0 %collective-permute-start.2 = (bf16[192,3072]{1,0:T(8,128)(2,1)S(1)}, bf16[192,3072]{1,0:T(8,128)(2,1)S(1)}, u32[]{:S(2)}, u32[]{:S(2)}) collective-permute-start(bf16[192,3072]{1,0:T(8,128)(2,1)S(1)} %fusion), channel_id=1, source_target_pairs={{0,32},{1,33},{2,34},{3,35},{4,36},{5,37},{6,38},{7,39},{8,40},{9,... | collective-permute-start | bytes 3538952 | tf_op jit(solution)/shard_map/ppermute | solution.py:439
  32.1 108.5 %factor.1 = (f32[48,1536]{1,0:T(8,128)}, f32[192,1536]{1,0:T(8,128)}, bf16[192,1536]{1,0:T(8,128)(2,1)}) custom-call(f32[48,1536]{1,0:T(8,128)} %bitcast.24, f32[192,1536]{1,0:T(8,128)} %bitcast.18), custom_call_target="tpu_custom_call" | custom-call | flops 70000001024 | bytes 20000000 | tf_op jit(solution)/shard_map/factor/pallas_call | solution.py:333
  140.6 2.4 %collective-permute-start = (bf16[192,1536]{1,0:T(8,128)(2,1)}, bf16[192,1536]{1,0:T(8,128)(2,1)S(1)}, u32[]{:S(2)}, u32[]{:S(2)}) collective-permute-start(bf16[192,1536]{1,0:T(8,128)(2,1)} %get-tuple-element.8.g_ref), channel_id=1, source_target_pairs={{0,32},{1,33},{2,34},{3,35},{4,36},{5,37},{6,38},{7,39},{8,40},{9,... | collective-permute-start | bytes 1769480 | tf_op jit(solution)/shard_map/ppermute | solution.py:442
  143.1 0.6 pad_add_fusion.1.pick
  143.7 1.0 dynamic-slice_subtract_fusion
  144.7 0.7 broadcast_subtract_fusion
  145.3 0.7 pad_add_fusion.pick
  146.0 1.4 dynamic-slice_subtract_fusion.2
  147.4 15.1 %assemble.2.base_ref = f32[256,4096]{1,0:T(8,128)} custom-call(s32[2]{0:T(128)} %pad_add_fusion.1.pick, bf16[192,1536]{1,0:T(8,128)(2,1)} %get-tuple-element.8.g_ref, bf16[6144,1536]{1,0:T(8,128)(2,1)} %all-gather.2.cloned.1.call-done.b_ref, f32[192,6144]{1,0:T(8,128)} %bitcast.17, s32[1,192]{1,0:T(1,128)} %get-tuple-element.11.rows_ref, ...), custom_call_target="tpu_custom_call" | custom-call | flops 5000000000 | bytes 20000000 | tf_op jit(solution)/shard_map/assemble/pallas_call | solution.py:382
  162.5 0.0 collective-permute-done.g_ref
  162.6 0.0 copy-start.2
  162.6 0.8 copy-done.3
  163.4 0.4 copy-done.2
  163.8 15.1 %assemble.3 = f32[256,4096]{1,0:T(8,128)} custom-call(s32[2]{0:T(128)} %pad_add_fusion.pick, bf16[192,1536]{1,0:T(8,128)(2,1)} %copy-done.3, bf16[6144,1536]{1,0:T(8,128)(2,1)} %all-gather.2.cloned.1.call-done.b_ref, bf16[192,3072]{1,0:T(8,128)(2,1)} %copy-done.2, s32[1,192]{1,0:T(1,128)} %get-tuple-element.12.rows_ref, ...), custom_call_target="tpu_custom_call", output_to_operand_aliasing={{}: (6, {})} | custom-call | flops 5000000000 | bytes 20000000 | tf_op jit(solution)/shard_map/assemble/pallas_call | solution.py:382
  178.8 0.7 copy.12
  179.5 1.0 copy.13
  (9 shorter events, 0.0 us)
Async XLA Ops:
  7.2 2.2 %copy-start = (f32[1,192,1536]{2,1,0:T(8,128)S(1)}, f32[1,192,1536]{2,1,0:T(8,128)}, u32[]{:S(2)}) copy-start(f32[1,192,1536]{2,1,0:T(8,128)} %param.6) | copy-start | bytes 3538948
  7.2 140.3 %all-gather.2.cloned.1.call-start = ((), (), s32[]{:S(2)}) async-start(), calls=%async_computation | async-start | bytes 19464192 | tf_op jit(solution)/shard_map/all_gather | solution.py:437
  8.6 0.7 collective-permute-start.1
  12.2 150.4 %collective-permute-start.2 = (bf16[192,3072]{1,0:T(8,128)(2,1)S(1)}, bf16[192,3072]{1,0:T(8,128)(2,1)S(1)}, u32[]{:S(2)}, u32[]{:S(2)}) collective-permute-start(bf16[192,3072]{1,0:T(8,128)(2,1)S(1)} %fusion), channel_id=1, source_target_pairs={{0,32},{1,33},{2,34},{3,35},{4,36},{5,37},{6,38},{7,39},{8,40},{9,... | collective-permute-start | bytes 3538952 | tf_op jit(solution)/shard_map/ppermute | solution.py:439
  140.6 21.9 %collective-permute-start = (bf16[192,1536]{1,0:T(8,128)(2,1)}, bf16[192,1536]{1,0:T(8,128)(2,1)S(1)}, u32[]{:S(2)}, u32[]{:S(2)}) collective-permute-start(bf16[192,1536]{1,0:T(8,128)(2,1)} %get-tuple-element.8.g_ref), channel_id=1, source_target_pairs={{0,32},{1,33},{2,34},{3,35},{4,36},{5,37},{6,38},{7,39},{8,40},{9,... | collective-permute-start | bytes 1769480 | tf_op jit(solution)/shard_map/ppermute | solution.py:442
  162.5 0.8 copy-start.3
  162.6 1.2 copy-start.2
  163.8 15.1 %copy-start.4 = (f32[48,1536]{1,0:T(8,128)S(1)}, f32[48,1536]{1,0:T(8,128)}, u32[]{:S(2)}) copy-start(f32[48,1536]{1,0:T(8,128)} %get-tuple-element.6) | copy-start | bytes 884740
  163.8 15.8 %copy-start.1 = (f32[192,1536]{1,0:T(8,128)S(1)}, f32[192,1536]{1,0:T(8,128)}, u32[]{:S(2)}) copy-start(f32[192,1536]{1,0:T(8,128)} %get-tuple-element.7) | copy-start | bytes 3538948
Sparse Core Ops, SparseCore 0:
  10.8 103.6 all-gather.1

commit v4 on v3

v4 whole, which is shorter than its diff:
```python
import functools

import jax
import jax.numpy as jnp
from jax import lax
from jax.experimental import pallas as pl
from jax.experimental.pallas import tpu as pltpu
from jax.sharding import PartitionSpec as P

DB = 128
PB = 256
f32 = jnp.float32
bf16 = jnp.bfloat16


def two_terms(value):
    high = value.astype(bf16)
    low = (value - high.astype(f32)).astype(bf16)
    return high, low


def nt(a, b):
    return lax.dot_general(a, b, (((1,), (1,)), ((), ())), preferred_element_type=f32)


def nn(a, b):
    return lax.dot_general(a, b, (((1,), (0,)), ((), ())), preferred_element_type=f32)


def left3(value):
    high, low = two_terms(value)
    return jnp.concatenate([high, high, low], axis=1)


def right3(value, axis=1):
    high, low = two_terms(value)
    return jnp.concatenate([high, low, high], axis=axis)


def nt3(a, b):
    return nt(left3(a), right3(b))


def nn3(a, b):
    return nn(left3(a), right3(b, 0))


def factor_corner(work, keep, pause, segments=2):
    count = DB // 8
    sub = lax.broadcasted_iota(jnp.int32, (8, DB), 0)

    def wide(row):
        return jnp.broadcast_to(row, (8, DB))

    def step(first, block, carry):
        start = pl.multiple_of(block * 8, 8)
        after = pl.multiple_of(start + 8, 8)
        before = pl.multiple_of(jnp.maximum(start - 8, 0), 8)
        started = jnp.where(block > 0, 1.0, 0.0).astype(f32)
        halves = (slice(0, DB), slice(DB, 2 * DB))
        rows = [work[pl.ds(start, 8), h] for h in halves]
        tile = [work[pl.ds(after, 8), h] for h in halves]
        past = [keep[pl.ds(before, 8), h] for h in halves]
        lane = jnp.zeros((8, DB), jnp.int32) + start
        lane_before = jnp.zeros((8, DB), jnp.int32) + before

        low = (first + 1) * 8
        if low < DB:
            left = work[low:DB, :DB]
            place = lax.broadcasted_iota(jnp.int32, left.shape, 1)
            depth = lax.broadcasted_iota(jnp.int32, left.shape, 0) + low
            chosen = (place >= start - 8) & (place < start) & (depth >= start + 16)
            left = jnp.where(chosen, left, 0.0)
            change = nn3(left, keep[...])

        for k in range(8):
            coef = jnp.take_along_axis(tile[0], lane_before + k, axis=1) * started
            if k == 0:
                drop = [coef * wide(past[s][k:k + 1]) for s in range(2)]
            else:
                drop = [drop[s] + coef * wide(past[s][k:k + 1]) for s in range(2)]
        tile = [tile[s] - drop[s] for s in range(2)]

        a = {}
        side_col = []
        for k in range(8):
            piece = jnp.take_along_axis(rows[0], lane + k, axis=1)
            for s in range(k, 8):
                a[s, k] = wide(piece[s:s + 1])
            side_col.append(jnp.take_along_axis(tile[0], lane + k, axis=1))
        r = []
        up = []
        for i in range(8):
            inv = lax.rsqrt(a[i, i])
            r.append(inv)
            for k in range(i + 1, 8):
                a[k, i] = a[k, i] * inv
            for k in range(i + 1, 8):
                for j in range(i + 1, k + 1):
                    a[k, j] = a[k, j] - a[k, i] * a[j, i]
            side_col[i] = side_col[i] * inv
            for k in range(i + 1, 8):
                side_col[k] = side_col[k] - a[k, i] * side_col[i]
            if i == 0:
                run = [[wide(rows[s][k:k + 1]) for k in range(8)] for s in range(2)]
            pair = []
            for s in range(2):
                value = run[s][i] * inv
                pair.append(value)
                for k in range(i + 1, 8):
                    run[s][k] = run[s][k] - a[k, i] * value
                tile[s] = tile[s] - side_col[i] * value
            up.append(pair)
        if low < DB:
            work[low:DB, :] = work[low:DB, :] - change
        for s in range(2):
            work[pl.ds(after, 8), halves[s]] = tile[s]
            value = up[0][s]
            for i in range(1, 8):
                value = jnp.where(sub == i, up[i][s], value)
            work[pl.ds(start, 8), halves[s]] = value
        back = [None] * 8
        for i in reversed(range(8)):
            pair = []
            for s in range(2):
                value = up[i][s]
                for k in range(i + 1, 8):
                    value = value - a[k, i] * back[k][s]
                pair.append(value * r[i])
            back[i] = pair
        for s in range(2):
            value = back[0][s]
            for i in range(1, 8):
                value = jnp.where(sub == i, back[i][s], value)
            keep[pl.ds(start, 8), halves[s]] = value
        return carry

    size = count // segments
    for seg in range(segments):
        lax.fori_loop(seg * size, (seg + 1) * size, lambda b, c, f=seg * size: step(f, b, c), 0)
        pause()


MESH = pl.DeviceIdType.MESH
RING = 4


class Place:
    def __init__(self):
        self.leaf = lax.axis_index("leaf")
        self.z = lax.axis_index("prow")
        pcol = lax.axis_index("pcol")
        self.x = pcol // 2
        self.core = pcol % 2
        self.flip = self.core == 1
        self.f = jnp.where(self.flip, self.z, self.x)
        self.s = jnp.where(self.flip, self.x, self.z)
        self.f_dev = [self.device(self.near(self.f, 1), self.s), self.device(self.near(self.f, -1), self.s)]
        self.s_dev = [self.device(self.f, self.near(self.s, 1)), self.device(self.f, self.near(self.s, -1))]
        self.twin = (self.leaf, self.z, self.x * 2 + 1 - self.core)
        self.far_dev = [self.device(self.near(self.f, 2), self.s), self.device(self.f, self.near(self.s, 2))]

    def near(self, v, d):
        return (v + d + RING) % RING

    def chip(self, fi, si):
        return jnp.where(self.flip, fi, si), jnp.where(self.flip, si, fi)

    def device(self, fi, si):
        zi, xi = self.chip(fi, si)
        return (self.leaf, zi, xi * 2 + self.core)


class Gather:
    OFFSETS = (0, -1, 1, 2)

    def __init__(self, place, source, view, rows, send, recv, needed=None, direct=False):
        self.place = place
        self.source = source
        self.view = view
        self.rows = rows
        self.send = send
        self.recv = recv
        self.needed = needed
        self.direct = direct
        self.started = []

    def window(self, fi, si, piece=None, twin=False):
        p = self.place
        zi, xi = p.chip(fi, si)
        slot = zi * 2 * RING + xi * 2 + ((1 - p.core) if twin else p.core)
        top = slot * self.rows
        part = self.rows // 2
        if piece is None:
            return self.view(pl.multiple_of(top, 8), self.rows)
        return self.view(pl.multiple_of(top + piece * part, 8), part)

    def under(self, fi, si, action):
        if self.needed is None:
            action()
        else:
            pl.when(self.needed(self.place.chip(fi, si)[0]))(action)

    def push(self, fi, si, src, dst, sem, dev):
        copy = pltpu.make_async_remote_copy(
            src_ref=src, dst_ref=dst, send_sem=self.send.at[len(self.started)],
            recv_sem=self.recv.at[sem], device_id=dev, device_id_type=MESH,
        )
        self.started.append((fi, si, copy))
        self.under(fi, si, copy.start)

    def arrived(self, fi, si, dst, sem):
        copy = pltpu.make_async_remote_copy(
            src_ref=dst, dst_ref=dst, send_sem=self.send.at[0],
            recv_sem=self.recv.at[sem], device_id=self.place.twin, device_id_type=MESH,
        )
        self.under(fi, si, copy.wait_recv)

    def f_sem(self, d):
        return d

    def s_sem(self, k, d):
        return 4 + 4 * k + d

    def c_sem(self, a, k):
        return 20 + 4 * a + k

    def pass_on(self, k, src, fi):
        p = self.place
        dst = self.window(fi, p.s)
        for d in range(2):
            self.push(fi, p.s, src, dst, self.s_sem(k, d), p.s_dev[d])
        if self.direct:
            self.push(fi, p.s, src, dst, self.s_sem(k, 2), p.far_dev[1])
        self.push(fi, p.s, src, dst, self.c_sem(0, k), p.twin)

    def begin(self):
        p = self.place
        for d in range(2):
            self.push(p.f, p.s, self.source, self.window(p.f, p.s), self.f_sem(d), p.f_dev[d])
        if self.direct:
            self.push(p.f, p.s, self.source, self.window(p.f, p.s), self.f_sem(2), p.far_dev[0])
        self.pass_on(0, self.source, p.f)

    def sides(self):
        p = self.place
        for d, off in ((0, -1), (1, 1)):
            fi = p.near(p.f, off)
            self.arrived(fi, p.s, self.window(fi, p.s), self.f_sem(d))
            if not self.direct:
                half = self.window(fi, p.s, d)
                self.push(fi, p.s, half, half, self.f_sem(2 + d), p.f_dev[d])
            self.pass_on(1 + d, self.window(fi, p.s), fi)

    def far(self):
        p = self.place
        fi = p.near(p.f, 2)
        if self.direct:
            self.arrived(fi, p.s, self.window(fi, p.s), self.f_sem(2))
        else:
            for d in range(2):
                self.arrived(fi, p.s, self.window(fi, p.s, d), self.f_sem(2 + d))
        self.pass_on(3, self.window(fi, p.s), fi)

    def second(self, k):
        p = self.place
        fi = p.near(p.f, self.OFFSETS[k])
        for d, off in ((0, -1), (1, 1)):
            si = p.near(p.s, off)
            self.arrived(fi, si, self.window(fi, si), self.s_sem(k, d))
            if not self.direct:
                half = self.window(fi, si, d)
                self.push(fi, si, half, half, self.s_sem(k, 2 + d), p.s_dev[d])
            whole = self.window(fi, si)
            self.push(fi, si, whole, whole, self.c_sem(1 + d, k), p.twin)

    def third(self, k):
        p = self.place
        fi = p.near(p.f, self.OFFSETS[k])
        si = p.near(p.s, 2)
        if self.direct:
            self.arrived(fi, si, self.window(fi, si), self.s_sem(k, 2))
        else:
            for d in range(2):
                self.arrived(fi, si, self.window(fi, si, d), self.s_sem(k, 2 + d))
        whole = self.window(fi, si)
        self.push(fi, si, whole, whole, self.c_sem(3, k), p.twin)

    def close(self):
        p = self.place
        for a in range(4):
            for b in range(4):
                fi = p.near(p.f, self.OFFSETS[a])
                si = p.near(p.s, self.OFFSETS[b])
                self.arrived(fi, si, self.window(fi, si, twin=True), self.c_sem(a, b))
        for fi, si, copy in self.started:
            self.under(fi, si, copy.wait_send)


CUTS = (0, 256, 512, 1024, 1536)


def factor_kernel(
    order, rows, a_ref, b_ref, l_ref, x_ref, g_ref,
    m, work, keep, inv, p_hi, p_lo, send, recv, extra,
):
    place = Place()
    held = l_ref.shape[0]
    eye = (lax.broadcasted_iota(jnp.int32, (DB, DB), 0) == lax.broadcasted_iota(jnp.int32, (DB, DB), 1)).astype(f32)
    low_mask = lax.broadcasted_iota(jnp.int32, (DB, DB), 0) >= lax.broadcasted_iota(jnp.int32, (DB, DB), 1)
    zero = jnp.zeros((DB, DB), f32)

    spot = place.z * 2 * RING + place.x * 2 + place.core
    own_rows = pl.ds(pl.multiple_of(spot * held, 8), held)

    groups = []
    needs = (None, None, lambda zi: zi >= 1, lambda zi: zi >= 2)
    for n in range(4):
        cols = slice(CUTS[n], CUTS[n + 1])
        groups.append(Gather(
            place, a_ref.at[:, cols],
            lambda top, size, cols=cols: m.at[pl.ds(top, size), cols],
            held, send.at[n], recv.at[n], needs[n], n < 2,
        ))
    mine = pltpu.make_async_copy(a_ref, m.at[own_rows, :], extra)

    barrier = pltpu.get_barrier_semaphore()
    peers = place.f_dev + place.s_dev + place.far_dev + [place.twin]
    for dev in peers:
        pl.semaphore_signal(barrier, inc=1, device_id=dev, device_id_type=MESH)
    mine.start()
    pl.semaphore_wait(barrier, len(peers))

    first, mid, late, last = groups
    first.begin()
    m[order:, :] = b_ref[...]
    keep[...] = jnp.zeros_like(keep)
    work[DB:, :] = jnp.zeros((8, 2 * DB), f32)
    first.sides()
    first.far()
    mid.begin()
    first.second(0)
    first.second(1)
    first.second(2)
    first.third(0)
    first.third(1)
    first.second(3)
    first.third(2)
    first.third(3)
    late.begin()
    last.begin()
    first.close()
    mine.wait()

    plan = {
        (0, 0): [mid.sides, mid.far],
        (0, 1): [lambda: mid.second(0), lambda: mid.second(1), lambda: mid.second(2), late.sides],
        (0, 2): [lambda: mid.third(0), lambda: mid.third(1), lambda: mid.second(3), lambda: late.second(0), late.far],
        (0, 3): [lambda: mid.third(2), lambda: mid.third(3), lambda: late.second(1), lambda: late.third(0)],
        (0, 4): [mid.close, last.sides],
        (0, 5): [lambda: late.second(2), lambda: late.third(1)],
        (1, 0): [lambda: late.second(3), lambda: late.third(2), lambda: last.second(0)],
        (1, 1): [lambda: late.third(3), last.far],
        (1, 2): [lambda: last.second(1), lambda: last.third(0)],
        (1, 4): [late.close],
        (1, 5): [lambda: last.second(2), lambda: last.third(1)],
        (2, 1): [lambda: last.second(3), lambda: last.third(2)],
        (2, 3): [lambda: last.third(3)],
        (2, 4): [last.close],
    }

    def update(q, j):
        j2 = j + PB
        qs = slice(q * PB, q * PB + PB)
        right = jnp.concatenate([p_hi[j:j2, qs], p_lo[j:j2, qs], p_hi[j:j2, qs]], axis=1)
        left = jnp.concatenate([p_hi[j:, qs], p_hi[j:, qs], p_lo[j:, qs]], axis=1)
        m[j:, j:j2] = m[j:, j:j2] - nt(left, right)

    for p in range(order // PB):
        count = [0]

        def pause():
            for action in plan.get((p, count[0]), ()):
                action()
            count[0] += 1

        c0 = p * PB
        c1 = c0 + DB
        c2 = c0 + PB
        work[:DB, :DB] = m[c0:c1, c0:c1]
        work[:DB, DB:] = eye
        factor_corner(work, keep, pause)
        l11 = jnp.where(low_mask, work[:DB, :DB].T, 0.0)
        i11 = work[:DB, DB:]
        l21 = nt3(m[c1:c2, c0:c1], i11)
        work[:DB, :DB] = m[c1:c2, c1:c2] - nt3(l21, l21)
        work[:DB, DB:] = eye
        m[c0:c1, c0:c1] = l11
        m[c0:c1, c1:c2] = zero
        m[c1:c2, c0:c1] = l21
        inv[c0:c1, :DB] = i11
        inv[c0:c1, DB:] = zero
        factor_corner(work, keep, pause)
        l22 = jnp.where(low_mask, work[:DB, :DB].T, 0.0)
        i22 = work[:DB, DB:]
        i21 = -nn3(i22, nn3(m[c1:c2, c0:c1], inv[c0:c1, :DB]))
        m[c1:c2, c1:c2] = l22
        inv[c1:c2, :DB] = i21
        inv[c1:c2, DB:] = i22
        panel = nt3(m[c2:, c0:c2], inv[c0:c2, :])
        m[c2:, c0:c2] = panel
        hi, lo = two_terms(panel)
        p_hi[c2:, c0:c2] = hi
        p_lo[c2:, c0:c2] = lo
        pause()
        for j in range(c2, order, PB):
            opens = max(CUTS[n] for n in range(4) if CUTS[n] <= j)
            due = {256: 0, 512: 1, 1024: 2}[opens]
            if p == due:
                for q in range(p):
                    update(q, j)
            if p >= due:
                update(p, j)
        pause()
    x_ref[...] = m[order:, :]
    own = m[own_rows, :]
    row_id = lax.broadcasted_iota(jnp.int32, own.shape, 0) + spot * held
    col_id = lax.broadcasted_iota(jnp.int32, own.shape, 1)
    l_ref[...] = jnp.where(col_id <= row_id, own, 0.0)
    for p in reversed(range(order // PB)):
        c0 = p * PB
        c2 = c0 + PB
        rhs = m[order:, c0:c2]
        if c2 < order:
            rhs = rhs - nn3(m[order:, c2:], m[c2:order, c0:c2])
        g = nn3(rhs, inv[c0:c2, :])
        m[order:, c0:c2] = g
        g_ref[:, c0:c2] = g.astype(bf16)


def factor(a, b):
    held, order = a.shape
    rows = b.shape[0]
    vm = pl.BlockSpec(memory_space=pltpu.VMEM)
    return pl.pallas_call(
        functools.partial(factor_kernel, order, rows),
        out_shape=(
            jax.ShapeDtypeStruct((held, order), f32),
            jax.ShapeDtypeStruct((rows, order), f32),
            jax.ShapeDtypeStruct((rows, order), bf16),
        ),
        in_specs=[vm, vm],
        out_specs=(vm, vm, vm),
        scratch_shapes=[
            pltpu.VMEM((order + rows, order), f32),
            pltpu.VMEM((DB + 8, 2 * DB), f32),
            pltpu.VMEM((DB, 2 * DB), f32),
            pltpu.VMEM((order, PB), f32),
            pltpu.VMEM((order + rows, order), bf16),
            pltpu.VMEM((order + rows, order), bf16),
            pltpu.SemaphoreType.DMA((4, 36)),
            pltpu.SemaphoreType.DMA((4, 36)),
            pltpu.SemaphoreType.DMA,
        ],
        compiler_params=pltpu.CompilerParams(
            vmem_limit_bytes=60 * 2**20, collective_id=0, has_side_effects=True
        ),
        cost_estimate=pl.CostEstimate(flops=100 * 10**9, bytes_accessed=2 * 10**7, transcendentals=0),
        name="factor",
    )(a, b)


def tables(rows_ref, cols_ref, height, width):
    rows = rows_ref.shape[1]
    cols = cols_ref.shape[2]
    row_table = (lax.broadcasted_iota(jnp.int32, (height, rows), 0) == rows_ref[...]).astype(bf16)
    col_table = (lax.broadcasted_iota(jnp.int32, (width, cols), 0) == cols_ref[0]).astype(bf16)
    return row_table, col_table


def send_kernel(pick, g_ref, b_ref, c_ref, out_ref):
    out_ref[...] = (c_ref[...] - nt(g_ref[...], b_ref[...])).astype(bf16)


def keep_kernel(pick, g_ref, b_ref, c_ref, rows_ref, cols_ref, base_ref, out_ref):
    row_table, col_table = tables(rows_ref, cols_ref, *base_ref.shape)
    high, low = two_terms(c_ref[...] - nt(g_ref[...], b_ref[...]))
    high = nt(high, col_table).astype(bf16)
    low = nt(low, col_table).astype(bf16)
    out_ref[...] = base_ref[...] + (nn(row_table, high) + nn(row_table, low))


def join_kernel(s_ref, rows_ref, cols_ref, base_ref, out_ref):
    row_table, col_table = tables(rows_ref, cols_ref, *base_ref.shape)
    out_ref[...] = base_ref[...] + nn(row_table, nt(s_ref[...], col_table).astype(bf16))


def cost(flops):
    return pl.CostEstimate(flops=flops, bytes_accessed=10**7, transcendentals=0)


def send_part(pick, g, b_all, c, wide, steps):
    rows, order = g.shape
    return pl.pallas_call(
        send_kernel,
        out_shape=jax.ShapeDtypeStruct((rows, wide * steps), bf16),
        grid_spec=pltpu.PrefetchScalarGridSpec(
            num_scalar_prefetch=1,
            grid=(steps,),
            in_specs=[
                pl.BlockSpec((rows, order), lambda t, pick: (0, 0)),
                pl.BlockSpec((wide, order), lambda t, pick: (pick[0] + t, 0)),
                pl.BlockSpec((rows, wide), lambda t, pick: (0, pick[0] + t)),
            ],
            out_specs=pl.BlockSpec((rows, wide), lambda t, pick: (0, t)),
        ),
        cost_estimate=cost(10**9),
        name="send_part",
    )(pick, g, b_all, c)


def keep_part(pick, g, b_all, c, row_link, col_link, base):
    steps, _, wide = col_link.shape
    rows, order = g.shape
    height, full = base.shape
    window = full // steps
    return pl.pallas_call(
        keep_kernel,
        out_shape=jax.ShapeDtypeStruct(base.shape, f32),
        grid_spec=pltpu.PrefetchScalarGridSpec(
            num_scalar_prefetch=1,
            grid=(steps,),
            in_specs=[
                pl.BlockSpec((rows, order), lambda t, pick: (0, 0)),
                pl.BlockSpec((wide, order), lambda t, pick: (pick[0] + t, 0)),
                pl.BlockSpec((rows, wide), lambda t, pick: (0, pick[0] + t)),
                pl.BlockSpec((1, rows), lambda t, pick: (0, 0)),
                pl.BlockSpec((1, 1, wide), lambda t, pick: (t, 0, 0)),
                pl.BlockSpec((height, window), lambda t, pick: (0, t)),
            ],
            out_specs=pl.BlockSpec((height, window), lambda t, pick: (0, t)),
        ),
        cost_estimate=cost(5 * 10**9),
        name="keep_part",
    )(pick, g, b_all, c, row_link, col_link, base)


def join_part(part, parts, got, row_link, col_link, base):
    steps, _, wide = col_link.shape
    rows = got.shape[0]
    height, full = base.shape
    window = full // steps
    count = steps // parts
    first = part * count
    return pl.pallas_call(
        join_kernel,
        out_shape=jax.ShapeDtypeStruct(base.shape, f32),
        grid=(count,),
        in_specs=[
            pl.BlockSpec((rows, wide), lambda t: (0, t)),
            pl.BlockSpec((1, rows), lambda t: (0, 0)),
            pl.BlockSpec((1, 1, wide), lambda t: (t + first, 0, 0)),
            pl.BlockSpec((height, window), lambda t: (0, t + first)),
        ],
        out_specs=pl.BlockSpec((height, window), lambda t: (0, t + first)),
        input_output_aliases={3: 0},
        cost_estimate=cost(10**9),
        name="join_part",
    )(got, row_link, col_link, base)


AXES = ("leaf", "prow", "pcol")


def local(front_pivot, front_lower, front_rest, parent_front, relation):
    position = lax.axis_index(("prow", "pcol"))
    leaf = lax.axis_index("leaf")
    spots = lax.axis_size("prow") * lax.axis_size("pcol")
    leaves = lax.axis_size("leaf")
    side = leaf % 2
    partner = leaf + 1 - 2 * side
    pivot_rows = front_pivot[0]
    lower_rows = front_lower[0]
    rest_rows = front_rest[0]
    base = parent_front[0]
    rows_here, child_order = rest_rows.shape
    half = child_order // 2
    height, parent_half = base.shape
    steps = 8
    wide = half // steps
    window = parent_half // steps


    mirror = [(one * spots + spot, (one ^ 1) * spots + spot) for one in range(leaves) for spot in range(spots)]
    b_all = lax.all_gather(lower_rows.astype(bf16), ("prow", "pcol"), axis=0, tiled=True)
    pivot_out, lower_out, g = factor(pivot_rows, lower_rows)

    def links(child):
        link = lax.dynamic_index_in_dim(relation, child, 0, keepdims=False)
        row_link = lax.dynamic_slice_in_dim(link, position * rows_here, rows_here, 0) - position * height
        col_link = lax.dynamic_slice_in_dim(link, side * half, half, 0) - side * parent_half
        col_link = col_link.reshape(steps, 1, wide) - jnp.arange(steps, dtype=jnp.int32)[:, None, None] * window
        return row_link[None], col_link

    row_own, col_own = links(leaf)
    row_sib, col_sib = links(partner)
    received = []
    parts = 2
    for part in range(parts):
        pick = jnp.full((1,), (1 - side) * steps + part * (steps // parts), jnp.int32)
        sent = send_part(pick, g, b_all, rest_rows, wide, steps // parts)
        received.append(lax.ppermute(sent, AXES, mirror))
    merged = keep_part(jnp.full((1,), side * steps, jnp.int32), g, b_all, rest_rows, row_own, col_own, base)
    for part in range(parts):
        merged = join_part(part, parts, received[part], row_sib, col_sib, merged)
    return (pivot_out[None], lower_out[None], merged[None])


def solution(mesh):
    spec = P("leaf", ("prow", "pcol"), None)
    return jax.shard_map(
        local,
        mesh=mesh,
        in_specs=(spec, spec, spec, spec, P()),
        out_specs=(spec, spec, spec),
        check_vma=False,
    )
```

time: 188 us -> 166 us (0.88)
  starting transfers between devices: 23.1 us -> 1.51 us
    ppermute x3 -> x2, starting transfers between devices: 23.1 us -> 1.47 us  [local(): received.append(lax.ppermute(sent, AXES, mirror))]
    pallas_call x2 -> x5, Pallas kernels: 30.2 us -> 35 us  [the longest x1 14.4 us: keep_part(): pl.pallas_call(keep_kernel, out_shape=jax.ShapeDtypeStruct(base.shape, f3...]
    pallas_call x1, Pallas kernels: 109 us -> 105 us  [factor(): pl.pallas_call(functools.partial(factor_kernel, order, rows), out_shape=(...]
  transfers between devices with their start and end apart: 4 -> 3, of which waited for: 0 -> 0; matrix products, arithmetic and copies ran while one was open for 3% -> 2% of each run, Pallas kernels for 66% -> 79%
where the time goes in v4:
time: 166 us; the launch traced here: 164 us
  Pallas kernels  140 us (84%)
  between operations  14.1 us (8%)
  other arithmetic  5.25 us (3%)
  local copies, waits for them, and re-layouts  3.36 us (2%)
    pallas_call x1, Pallas kernels, factor(): pl.pallas_call(functools.partial(factor_kernel, order, rows), out_shape=(...  105 us
    pallas_call x1, Pallas kernels, keep_part(): pl.pallas_call(keep_kernel, out_shape=jax.ShapeDtypeStruct(base.shape, f3...  14.4 us
    pallas_call x2, Pallas kernels, send_part(): pl.pallas_call(send_kernel, out_shape=jax.ShapeDtypeStruct((rows, wide *...  10.8 us
    pallas_call x2, Pallas kernels, join_part(): pl.pallas_call(join_kernel, out_shape=jax.ShapeDtypeStruct(base.shape, f3...  9.74 us
    unnamed x10, local copies, waits for them, and re-layouts  3.36 us
  transfers between devices with their start and end apart: 3, of which 0 were waited for; matrix products, arithmetic and copies ran while one was open for 2% of the time, Pallas kernels for 79%

profile of v4, /device:TPU:1, one launch (start us, length us, event | category | flops | bytes accessed | tf_op | source)
XLA Modules:
  0.0 164.1 jit_solution(5934295404231878642)
XLA Ops:
  7.2 0.0 all-gather.2.cloned.1.call-start
  7.2 2.1 %bitcast_convert_fusion = bf16[192,1536]{1,0:T(8,128)(2,1)} fusion(f32[1,192,1536]{2,1,0:T(8,128)} %param.6), kind=kLoop, calls=%fused_computation.7 | loop fusion | flops 294912 | bytes 1769472 | tf_op jit(solution)/shard_map/convert_element_type | solution.py:595
  9.4 0.0 all-gather.2.cloned.1.call-update
  9.4 1.0 dynamic-slice_subtract_fusion
  10.4 0.7 broadcast_subtract_fusion
  11.1 104.8 %factor.1 = (f32[48,1536]{1,0:T(8,128)}, f32[192,1536]{1,0:T(8,128)}, bf16[192,1536]{1,0:T(8,128)(2,1)}) custom-call(f32[48,1536]{1,0:T(8,128)} %bitcast.23, f32[192,1536]{1,0:T(8,128)} %bitcast.18), custom_call_target="tpu_custom_call" | custom-call | flops 99999997952 | bytes 20000000 | tf_op jit(solution)/shard_map/factor/pallas_call | solution.py:445
  116.0 0.0 all-gather.2.cloned.1.call-done.b_ref
  116.0 5.4 %send_part.3 = bf16[192,1536]{1,0:T(8,128)(2,1)} custom-call(s32[1]{0:T(128)} %bitcast.7.pick, bf16[192,1536]{1,0:T(8,128)(2,1)} %get-tuple-element.8.g_ref, bf16[6144,1536]{1,0:T(8,128)(2,1)} %all-gather.2.cloned.1.call-done.b_ref, f32[192,6144]{1,0:T(8,128)} %bitcast.13), custom_call_target="tpu_custom_call" | custom-call | flops 1000000000 | bytes 10000000 | tf_op jit(solution)/shard_map/send_part/pallas_call | solution.py:504
  121.4 1.2 collective-permute-start.1
  122.6 5.4 %send_part.2 = bf16[192,1536]{1,0:T(8,128)(2,1)} custom-call(s32[1]{0:T(128)} %bitcast.4.pick, bf16[192,1536]{1,0:T(8,128)(2,1)} %get-tuple-element.8.g_ref, bf16[6144,1536]{1,0:T(8,128)(2,1)} %all-gather.2.cloned.1.call-done.b_ref, f32[192,6144]{1,0:T(8,128)} %bitcast.14), custom_call_target="tpu_custom_call" | custom-call | flops 1000000000 | bytes 10000000 | tf_op jit(solution)/shard_map/send_part/pallas_call | solution.py:504
  128.0 0.3 collective-permute-start
  128.3 1.4 dynamic-slice_subtract_fusion.2
  129.7 14.4 %keep_part.1.base_ref = f32[256,4096]{1,0:T(8,128)} custom-call(s32[1]{0:T(128)} %bitcast.8.pick, bf16[192,1536]{1,0:T(8,128)(2,1)} %get-tuple-element.8.g_ref, bf16[6144,1536]{1,0:T(8,128)(2,1)} %all-gather.2.cloned.1.call-done.b_ref, f32[192,6144]{1,0:T(8,128)} %bitcast.15, s32[1,192]{1,0:T(1,128)} %get-tuple-element.11.rows_ref, ...), custom_call_target="tpu_custom_call" | custom-call | flops 5000000000 | bytes 10000000 | tf_op jit(solution)/shard_map/keep_part/pallas_call | solution.py:527
  144.1 0.0 collective-permute-done.1.s_ref
  144.1 0.8 copy-done.2
  144.9 4.9 %join_part.2.base_ref = f32[256,4096]{1,0:T(8,128)} custom-call(bf16[192,1536]{1,0:T(8,128)(2,1)} %copy-done.2, s32[1,192]{1,0:T(1,128)} %get-tuple-element.12.rows_ref, s32[8,1,384]{2,1,0:T(1,128)} %get-tuple-element.14.cols_ref, f32[256,4096]{1,0:T(8,128)} %keep_part.1.base_ref), custom_call_target="tpu_custom_call", output_to_operand_aliasing={{}: (3, {})} | custom-call | flops 1000000000 | bytes 10000000 | tf_op jit(solution)/shard_map/join_part/pallas_call | solution.py:555
  149.8 0.0 collective-permute-done.s_ref
  149.8 0.0 copy-start.1
  149.8 0.8 copy-done.1
  150.6 4.9 %join_part.3 = f32[256,4096]{1,0:T(8,128)} custom-call(bf16[192,1536]{1,0:T(8,128)(2,1)} %copy-done.1, s32[1,192]{1,0:T(1,128)} %get-tuple-element.12.rows_ref, s32[8,1,384]{2,1,0:T(1,128)} %get-tuple-element.14.cols_ref, f32[256,4096]{1,0:T(8,128)} %join_part.2.base_ref), custom_call_target="tpu_custom_call", output_to_operand_aliasing={{}: (3, {})} | custom-call | flops 1000000000 | bytes 10000000 | tf_op jit(solution)/shard_map/join_part/pallas_call | solution.py:555
  155.5 0.0 copy-done.3
  155.5 0.7 copy.14
  156.2 0.0 copy-done
  156.2 1.0 copy.15
  (4 shorter events, 0.0 us)
Async XLA Ops:
  7.2 108.8 %all-gather.2.cloned.1.call-start = ((), (), s32[]{:S(2)}) async-start(), calls=%async_computation | async-start | bytes 19464192 | tf_op jit(solution)/shard_map/all_gather | solution.py:595
  121.4 22.7 %collective-permute-start.1 = (bf16[192,1536]{1,0:T(8,128)(2,1)}, bf16[192,1536]{1,0:T(8,128)(2,1)S(1)}, u32[]{:S(2)}, u32[]{:S(2)}) collective-permute-start(bf16[192,1536]{1,0:T(8,128)(2,1)} %send_part.3), channel_id=1, source_target_pairs={{0,32},{1,33},{2,34},{3,35},{4,36},{5,37},{6,38},{7,39},{8,40},{9,... | collective-permute-start | bytes 1769480 | tf_op jit(solution)/shard_map/ppermute | solution.py:612
  128.0 21.8 %collective-permute-start = (bf16[192,1536]{1,0:T(8,128)(2,1)}, bf16[192,1536]{1,0:T(8,128)(2,1)S(1)}, u32[]{:S(2)}, u32[]{:S(2)}) collective-permute-start(bf16[192,1536]{1,0:T(8,128)(2,1)} %send_part.2), channel_id=1, source_target_pairs={{0,32},{1,33},{2,34},{3,35},{4,36},{5,37},{6,38},{7,39},{8,40},{9,... | collective-permute-start | bytes 1769480 | tf_op jit(solution)/shard_map/ppermute | solution.py:612
  144.1 0.8 copy-start.2
  149.8 5.7 %copy-start.3 = (f32[48,1536]{1,0:T(8,128)S(1)}, f32[48,1536]{1,0:T(8,128)}, u32[]{:S(2)}) copy-start(f32[48,1536]{1,0:T(8,128)} %get-tuple-element.6) | copy-start | bytes 884740
  149.8 6.4 %copy-start = (f32[192,1536]{1,0:T(8,128)S(1)}, f32[192,1536]{1,0:T(8,128)}, u32[]{:S(2)}) copy-start(f32[192,1536]{1,0:T(8,128)} %get-tuple-element.7) | copy-start | bytes 3538948
  149.8 0.8 copy-start.1
Sparse Core Ops, SparseCore 0:
  10.8 91.4 all-gather.1

commit v5 on v4

--- a/solution.py
+++ b/solution.py
@@ -124,7 +124,7 @@
             pair = []
             for s in range(2):
                 value = up[i][s]
-                for k in range(i + 1, 8):
+                for k in reversed(range(i + 1, 8)):
                     value = value - a[k, i] * back[k][s]
                 pair.append(value * r[i])
             back[i] = pair
@@ -320,7 +320,7 @@
         groups.append(Gather(
             place, a_ref.at[:, cols],
             lambda top, size, cols=cols: m.at[pl.ds(top, size), cols],
-            held, send.at[n], recv.at[n], needs[n], n < 2,
+            held, send.at[n], recv.at[n], needs[n], True,
         ))
     mine = pltpu.make_async_copy(a_ref, m.at[own_rows, :], extra)
 
@@ -470,11 +470,14 @@
     )(a, b)
 
 
-def tables(rows_ref, cols_ref, height, width):
+GROUP = 2
+
+
+def tables(rows_ref, cols_ref, part, height, width):
     rows = rows_ref.shape[1]
     cols = cols_ref.shape[2]
     row_table = (lax.broadcasted_iota(jnp.int32, (height, rows), 0) == rows_ref[...]).astype(bf16)
-    col_table = (lax.broadcasted_iota(jnp.int32, (width, cols), 0) == cols_ref[0]).astype(bf16)
+    col_table = (lax.broadcasted_iota(jnp.int32, (width, cols), 0) == cols_ref[part]).astype(bf16)
     return row_table, col_table
 
 
@@ -483,16 +486,28 @@
 
 
 def keep_kernel(pick, g_ref, b_ref, c_ref, rows_ref, cols_ref, base_ref, out_ref):
-    row_table, col_table = tables(rows_ref, cols_ref, *base_ref.shape)
-    high, low = two_terms(c_ref[...] - nt(g_ref[...], b_ref[...]))
-    high = nt(high, col_table).astype(bf16)
-    low = nt(low, col_table).astype(bf16)
-    out_ref[...] = base_ref[...] + (nn(row_table, high) + nn(row_table, low))
+    height, width = base_ref.shape
+    width //= GROUP
+    wide = cols_ref.shape[2]
+    schur = c_ref[...] - nt(g_ref[...], b_ref[...])
+    for part in range(GROUP):
+        row_table, col_table = tables(rows_ref, cols_ref, part, height, width)
+        high, low = two_terms(schur[:, part * wide:part * wide + wide])
+        high = nt(high, col_table).astype(bf16)
+        low = nt(low, col_table).astype(bf16)
+        here = slice(part * width, part * width + width)
+        out_ref[:, here] = base_ref[:, here] + (nn(row_table, high) + nn(row_table, low))
 
 
 def join_kernel(s_ref, rows_ref, cols_ref, base_ref, out_ref):
-    row_table, col_table = tables(rows_ref, cols_ref, *base_ref.shape)
-    out_ref[...] = base_ref[...] + nn(row_table, nt(s_ref[...], col_table).astype(bf16))
+    height, width = base_ref.shape
+    width //= GROUP
+    wide = cols_ref.shape[2]
+    for part in range(GROUP):
+        row_table, col_table = tables(rows_ref, cols_ref, part, height, width)
+        here = slice(part * width, part * width + width)
+        spread = nt(s_ref[:, part * wide:part * wide + wide], col_table).astype(bf16)
+        out_ref[:, here] = base_ref[:, here] + nn(row_table, spread)
 
 
 def cost(flops):
@@ -523,7 +538,9 @@
     steps, _, wide = col_link.shape
     rows, order = g.shape
     height, full = base.shape
-    window = full // steps
+    window = full // steps * GROUP
+    steps //= GROUP
+    block = wide * GROUP
     return pl.pallas_call(
         keep_kernel,
         out_shape=jax.ShapeDtypeStruct(base.shape, f32),
@@ -532,10 +549,10 @@
             grid=(steps,),
             in_specs=[
                 pl.BlockSpec((rows, order), lambda t, pick: (0, 0)),
-                pl.BlockSpec((wide, order), lambda t, pick: (pick[0] + t, 0)),
-                pl.BlockSpec((rows, wide), lambda t, pick: (0, pick[0] + t)),
+                pl.BlockSpec((block, order), lambda t, pick: (pick[0] + t, 0)),
+                pl.BlockSpec((rows, block), lambda t, pick: (0, pick[0] + t)),
                 pl.BlockSpec((1, rows), lambda t, pick: (0, 0)),
-                pl.BlockSpec((1, 1, wide), lambda t, pick: (t, 0, 0)),
+                pl.BlockSpec((GROUP, 1, wide), lambda t, pick: (t, 0, 0)),
                 pl.BlockSpec((height, window), lambda t, pick: (0, t)),
             ],
             out_specs=pl.BlockSpec((height, window), lambda t, pick: (0, t)),
@@ -549,7 +566,9 @@
     steps, _, wide = col_link.shape
     rows = got.shape[0]
     height, full = base.shape
-    window = full // steps
+    window = full // steps * GROUP
+    steps //= GROUP
+    block = wide * GROUP
     count = steps // parts
     first = part * count
     return pl.pallas_call(
@@ -557,9 +576,9 @@
         out_shape=jax.ShapeDtypeStruct(base.shape, f32),
         grid=(count,),
         in_specs=[
-            pl.BlockSpec((rows, wide), lambda t: (0, t)),
+            pl.BlockSpec((rows, block), lambda t: (0, t)),
             pl.BlockSpec((1, rows), lambda t: (0, 0)),
-            pl.BlockSpec((1, 1, wide), lambda t: (t + first, 0, 0)),
+            pl.BlockSpec((GROUP, 1, wide), lambda t: (t + first, 0, 0)),
             pl.BlockSpec((height, window), lambda t: (0, t + first)),
         ],
         out_specs=pl.BlockSpec((height, window), lambda t: (0, t + first)),
@@ -607,10 +626,10 @@
     received = []
     parts = 2
     for part in range(parts):
-        pick = jnp.full((1,), (1 - side) * steps + part * (steps // parts), jnp.int32)
-        sent = send_part(pick, g, b_all, rest_rows, wide, steps // parts)
+        pick = jnp.full((1,), ((1 - side) * steps + part * (steps // parts)) // GROUP, jnp.int32)
+        sent = send_part(pick, g, b_all, rest_rows, wide * GROUP, steps // parts // GROUP)
         received.append(lax.ppermute(sent, AXES, mirror))
-    merged = keep_part(jnp.full((1,), side * steps, jnp.int32), g, b_all, rest_rows, row_own, col_own, base)
+    merged = keep_part(jnp.full((1,), side * steps // GROUP, jnp.int32), g, b_all, rest_rows, row_own, col_own, base)
     for part in range(parts):
         merged = join_part(part, parts, received[part], row_sib, col_sib, merged)
     return (pivot_out[None], lower_out[None], merged[None])

time: 166 us -> 158 us (0.952)
  Pallas kernels: 140 us -> 130 us
  waiting for transfers between devices: 0.04 us -> 3.3 us
    pallas_call x1, Pallas kernels: 105 us -> 101 us  [factor(): pl.pallas_call(functools.partial(factor_kernel, order, rows), out_shape=(...]
    ppermute x2, waiting for transfers between devices: 0.01 us -> 3.26 us  [local(): received.append(lax.ppermute(sent, AXES, mirror))]
    pallas_call x1, Pallas kernels: 14.4 us -> 12 us  [keep_part(): pl.pallas_call(keep_kernel, out_shape=jax.ShapeDtypeStruct(base.shape, f3...]
    pallas_call x2, Pallas kernels: 9.74 us -> 7.91 us  [join_part(): pl.pallas_call(join_kernel, out_shape=jax.ShapeDtypeStruct(base.shape, f3...]
    pallas_call x2, Pallas kernels: 10.8 us -> 9.07 us  [send_part(): pl.pallas_call(send_kernel, out_shape=jax.ShapeDtypeStruct((rows, wide *...]
  transfers between devices with their start and end apart: 3 -> 3, of which waited for: 0 -> 1; matrix products, arithmetic and copies ran while one was open for 2% -> 2% of each run, Pallas kernels for 79% -> 77%
where the time goes in v5:
time: 158 us; the launch traced here: 157 us
  Pallas kernels  130 us (82%)
  between operations  14.2 us (9%)
  other arithmetic  5.25 us (3%)
  local copies, waits for them, and re-layouts  3.37 us (2%)
  waiting for transfers between devices  3.3 us (2%)
    pallas_call x1, Pallas kernels, factor(): pl.pallas_call(functools.partial(factor_kernel, order, rows), out_shape=(...  101 us
    pallas_call x1, Pallas kernels, keep_part(): pl.pallas_call(keep_kernel, out_shape=jax.ShapeDtypeStruct(base.shape, f3...  12 us
    pallas_call x2, Pallas kernels, send_part(): pl.pallas_call(send_kernel, out_shape=jax.ShapeDtypeStruct((rows, wide *...  9.07 us
    pallas_call x2, Pallas kernels, join_part(): pl.pallas_call(join_kernel, out_shape=jax.ShapeDtypeStruct(base.shape, f3...  7.91 us
    unnamed x10, local copies, waits for them, and re-layouts  3.37 us
    ppermute x2, waiting for transfers between devices, local(): received.append(lax.ppermute(sent, AXES, mirror))  3.26 us
  transfers between devices with their start and end apart: 3, of which 1 were waited for; matrix products, arithmetic and copies ran while one was open for 2% of the time, Pallas kernels for 77%

profile of v5, /device:TPU:1, one launch (start us, length us, event | category | flops | bytes accessed | tf_op | source)
XLA Modules:
  0.0 157.3 jit_solution(16483882377068550401)
XLA Ops:
  7.2 0.0 all-gather.2.cloned.1.call-start
  7.2 2.1 %bitcast_convert_fusion = bf16[192,1536]{1,0:T(8,128)(2,1)} fusion(f32[1,192,1536]{2,1,0:T(8,128)} %param.6), kind=kLoop, calls=%fused_computation.7 | loop fusion | flops 294912 | bytes 1769472 | tf_op jit(solution)/shard_map/convert_element_type | solution.py:614
  9.4 0.0 all-gather.2.cloned.1.call-update
  9.5 1.0 dynamic-slice_subtract_fusion
  10.5 0.7 broadcast_subtract_fusion
  11.2 100.7 %factor.1 = (f32[48,1536]{1,0:T(8,128)}, f32[192,1536]{1,0:T(8,128)}, bf16[192,1536]{1,0:T(8,128)(2,1)}) custom-call(f32[48,1536]{1,0:T(8,128)} %bitcast.23, f32[192,1536]{1,0:T(8,128)} %bitcast.18), custom_call_target="tpu_custom_call" | custom-call | flops 99999997952 | bytes 20000000 | tf_op jit(solution)/shard_map/factor/pallas_call | solution.py:445
  111.9 0.0 all-gather.2.cloned.1.call-done.b_ref
  112.0 4.6 %send_part.3 = bf16[192,1536]{1,0:T(8,128)(2,1)} custom-call(s32[1]{0:T(128)} %bitcast.7.pick, bf16[192,1536]{1,0:T(8,128)(2,1)} %get-tuple-element.8.g_ref, bf16[6144,1536]{1,0:T(8,128)(2,1)} %all-gather.2.cloned.1.call-done.b_ref, f32[192,6144]{1,0:T(8,128)} %bitcast.13), custom_call_target="tpu_custom_call" | custom-call | flops 1000000000 | bytes 10000000 | tf_op jit(solution)/shard_map/send_part/pallas_call | solution.py:519
  116.5 1.2 collective-permute-start.1
  117.7 4.5 %send_part.2 = bf16[192,1536]{1,0:T(8,128)(2,1)} custom-call(s32[1]{0:T(128)} %bitcast.4.pick, bf16[192,1536]{1,0:T(8,128)(2,1)} %get-tuple-element.8.g_ref, bf16[6144,1536]{1,0:T(8,128)(2,1)} %all-gather.2.cloned.1.call-done.b_ref, f32[192,6144]{1,0:T(8,128)} %bitcast.14), custom_call_target="tpu_custom_call" | custom-call | flops 1000000000 | bytes 10000000 | tf_op jit(solution)/shard_map/send_part/pallas_call | solution.py:519
  122.2 0.3 collective-permute-start
  122.5 1.4 dynamic-slice_subtract_fusion.2
  123.9 12.0 %keep_part.1.base_ref = f32[256,4096]{1,0:T(8,128)} custom-call(s32[1]{0:T(128)} %bitcast.8.pick, bf16[192,1536]{1,0:T(8,128)(2,1)} %get-tuple-element.8.g_ref, bf16[6144,1536]{1,0:T(8,128)(2,1)} %all-gather.2.cloned.1.call-done.b_ref, f32[192,6144]{1,0:T(8,128)} %bitcast.15, s32[1,192]{1,0:T(1,128)} %get-tuple-element.11.rows_ref, ...), custom_call_target="tpu_custom_call" | custom-call | flops 5000000000 | bytes 10000000 | tf_op jit(solution)/shard_map/keep_part/pallas_call | solution.py:544
  135.9 0.0 collective-permute-done.1.s_ref
  135.9 0.0 copy-start.2
  135.9 0.8 copy-done.2
  136.8 4.0 %join_part.2.base_ref = f32[256,4096]{1,0:T(8,128)} custom-call(bf16[192,1536]{1,0:T(8,128)(2,1)} %copy-done.2, s32[1,192]{1,0:T(1,128)} %get-tuple-element.12.rows_ref, s32[8,1,384]{2,1,0:T(1,128)} %get-tuple-element.14.cols_ref, f32[256,4096]{1,0:T(8,128)} %keep_part.1.base_ref), custom_call_target="tpu_custom_call", output_to_operand_aliasing={{}: (3, {})} | custom-call | flops 1000000000 | bytes 10000000 | tf_op jit(solution)/shard_map/join_part/pallas_call | solution.py:574
  140.7 3.3 %collective-permute-done.s_ref = bf16[192,1536]{1,0:T(8,128)(2,1)S(1)} collective-permute-done((bf16[192,1536]{1,0:T(8,128)(2,1)}, bf16[192,1536]{1,0:T(8,128)(2,1)S(1)}, u32[]{:S(2)}, u32[]{:S(2)}) %collective-permute-start) | collective-permute-done | bytes 589856 | tf_op jit(solution)/shard_map/ppermute | solution.py:631
  144.0 0.8 copy-done.1
  144.8 4.0 %join_part.3 = f32[256,4096]{1,0:T(8,128)} custom-call(bf16[192,1536]{1,0:T(8,128)(2,1)} %copy-done.1, s32[1,192]{1,0:T(1,128)} %get-tuple-element.12.rows_ref, s32[8,1,384]{2,1,0:T(1,128)} %get-tuple-element.14.cols_ref, f32[256,4096]{1,0:T(8,128)} %join_part.2.base_ref), custom_call_target="tpu_custom_call", output_to_operand_aliasing={{}: (3, {})} | custom-call | flops 1000000000 | bytes 10000000 | tf_op jit(solution)/shard_map/join_part/pallas_call | solution.py:574
  148.8 0.0 copy-done.3
  148.8 0.7 copy.14
  149.5 0.0 copy-done
  149.5 1.0 copy.15
  (4 shorter events, 0.0 us)
Async XLA Ops:
  7.2 104.8 %all-gather.2.cloned.1.call-start = ((), (), s32[]{:S(2)}) async-start(), calls=%async_computation | async-start | bytes 19464192 | tf_op jit(solution)/shard_map/all_gather | solution.py:614
  116.5 19.4 %collective-permute-start.1 = (bf16[192,1536]{1,0:T(8,128)(2,1)}, bf16[192,1536]{1,0:T(8,128)(2,1)S(1)}, u32[]{:S(2)}, u32[]{:S(2)}) collective-permute-start(bf16[192,1536]{1,0:T(8,128)(2,1)} %send_part.3), channel_id=1, source_target_pairs={{0,32},{1,33},{2,34},{3,35},{4,36},{5,37},{6,38},{7,39},{8,40},{9,... | collective-permute-start | bytes 1769480 | tf_op jit(solution)/shard_map/ppermute | solution.py:631
  122.2 21.8 %collective-permute-start = (bf16[192,1536]{1,0:T(8,128)(2,1)}, bf16[192,1536]{1,0:T(8,128)(2,1)S(1)}, u32[]{:S(2)}, u32[]{:S(2)}) collective-permute-start(bf16[192,1536]{1,0:T(8,128)(2,1)} %send_part.2), channel_id=1, source_target_pairs={{0,32},{1,33},{2,34},{3,35},{4,36},{5,37},{6,38},{7,39},{8,40},{9,... | collective-permute-start | bytes 1769480 | tf_op jit(solution)/shard_map/ppermute | solution.py:631
  135.9 0.8 copy-start.2
  140.7 8.0 %copy-start.3 = (f32[48,1536]{1,0:T(8,128)S(1)}, f32[48,1536]{1,0:T(8,128)}, u32[]{:S(2)}) copy-start(f32[48,1536]{1,0:T(8,128)} %get-tuple-element.6) | copy-start | bytes 884740
  140.7 8.8 %copy-start = (f32[192,1536]{1,0:T(8,128)S(1)}, f32[192,1536]{1,0:T(8,128)}, u32[]{:S(2)}) copy-start(f32[192,1536]{1,0:T(8,128)} %get-tuple-element.7) | copy-start | bytes 3538948
  144.0 0.8 copy-start.1
Sparse Core Ops, SparseCore 0:
  10.8 94.2 all-gather.1

commit v6 on v5

--- a/solution.py
+++ b/solution.py
@@ -630,8 +630,11 @@
         sent = send_part(pick, g, b_all, rest_rows, wide * GROUP, steps // parts // GROUP)
         received.append(lax.ppermute(sent, AXES, mirror))
     merged = keep_part(jnp.full((1,), side * steps // GROUP, jnp.int32), g, b_all, rest_rows, row_own, col_own, base)
-    for part in range(parts):
+    for part in reversed(range(parts)):
         merged = join_part(part, parts, received[part], row_sib, col_sib, merged)
+    pivot_out, lower_out, sent = lax.optimization_barrier((pivot_out, lower_out, sent))
+    pivot_out = jnp.where(position >= 0, pivot_out, 0.0)
+    lower_out = jnp.where(position >= 0, lower_out, 0.0)
     return (pivot_out[None], lower_out[None], merged[None])
 
 

time: 158 us -> 158 us (level)
  other arithmetic: 5.25 us -> 7.12 us
  local copies, waits for them, and re-layouts: 3.37 us -> 1.65 us
    broadcast_in_dim x0 -> x2, other arithmetic: none -> 1.83 us  [local(): return (pivot_out[None], lower_out[None], merged[None])]
    unnamed x10 -> x8, local copies, waits for them, and re-layouts: 3.37 us -> 1.65 us
  transfers between devices with their start and end apart: 3 -> 3, of which waited for: 1 -> 1; matrix products, arithmetic and copies ran while one was open for 2% -> 3% of each run, Pallas kernels for 77% -> 77%
where the time goes in v6:
time: 158 us; the launch traced here: 157 us
  Pallas kernels  130 us (82%)
  between operations  14.2 us (9%)
  other arithmetic  7.12 us (5%)
  waiting for transfers between devices  2.64 us (2%)
  local copies, waits for them, and re-layouts  1.65 us (1%)
    pallas_call x1, Pallas kernels, factor(): pl.pallas_call(functools.partial(factor_kernel, order, rows), out_shape=(...  101 us
    pallas_call x1, Pallas kernels, keep_part(): pl.pallas_call(keep_kernel, out_shape=jax.ShapeDtypeStruct(base.shape, f3...  12 us
    pallas_call x2, Pallas kernels, send_part(): pl.pallas_call(send_kernel, out_shape=jax.ShapeDtypeStruct((rows, wide *...  9.21 us
    pallas_call x2, Pallas kernels, join_part(): pl.pallas_call(join_kernel, out_shape=jax.ShapeDtypeStruct(base.shape, f3...  7.91 us
  transfers between devices with their start and end apart: 3, of which 1 were waited for; matrix products, arithmetic and copies ran while one was open for 3% of the time, Pallas kernels for 77%

profile of v6, /device:TPU:1, one launch (start us, length us, event | category | flops | bytes accessed | tf_op | source)
XLA Modules:
  0.0 157.4 jit_solution(1431671727414819084)
XLA Ops:
  7.2 0.0 all-gather.2.cloned.1.call-start
  7.2 2.1 %bitcast_convert_fusion = bf16[192,1536]{1,0:T(8,128)(2,1)} fusion(f32[1,192,1536]{2,1,0:T(8,128)} %param.6), kind=kLoop, calls=%fused_computation.9 | loop fusion | flops 294912 | bytes 1769472 | tf_op jit(solution)/shard_map/convert_element_type | solution.py:614
  9.4 0.0 all-gather.2.cloned.1.call-update
  9.5 1.4 dynamic-slice_subtract_fusion.2
  10.9 1.0 dynamic-slice_subtract_fusion
  11.9 0.7 broadcast_subtract_fusion
  12.6 101.2 %factor.1 = (f32[48,1536]{1,0:T(8,128)}, f32[192,1536]{1,0:T(8,128)}, bf16[192,1536]{1,0:T(8,128)(2,1)}) custom-call(f32[48,1536]{1,0:T(8,128)} %bitcast.23, f32[192,1536]{1,0:T(8,128)} %bitcast.20), custom_call_target="tpu_custom_call" | custom-call | flops 99999997952 | bytes 20000000 | tf_op jit(solution)/shard_map/factor/pallas_call | solution.py:445
  113.8 0.0 all-gather.2.cloned.1.call-done.b_ref
  113.8 4.6 %send_part.2 = bf16[192,1536]{1,0:T(8,128)(2,1)} custom-call(s32[1]{0:T(128)} %bitcast.2.pick, bf16[192,1536]{1,0:T(8,128)(2,1)} %get-tuple-element.10.g_ref, bf16[6144,1536]{1,0:T(8,128)(2,1)} %all-gather.2.cloned.1.call-done.b_ref, f32[192,6144]{1,0:T(8,128)} %bitcast.15), custom_call_target="tpu_custom_call" | custom-call | flops 1000000000 | bytes 10000000 | tf_op jit(solution)/shard_map/send_part/pallas_call | solution.py:519
  118.4 1.3 collective-permute-start.1
  119.7 0.0 copy-start
  119.7 4.6 %send_part.3 = bf16[192,1536]{1,0:T(8,128)(2,1)} custom-call(s32[1]{0:T(128)} %bitcast.6.pick, bf16[192,1536]{1,0:T(8,128)(2,1)} %get-tuple-element.10.g_ref, bf16[6144,1536]{1,0:T(8,128)(2,1)} %all-gather.2.cloned.1.call-done.b_ref, f32[192,6144]{1,0:T(8,128)} %bitcast.16), custom_call_target="tpu_custom_call" | custom-call | flops 1000000000 | bytes 10000000 | tf_op jit(solution)/shard_map/send_part/pallas_call | solution.py:519
  124.4 0.2 collective-permute-start
  124.5 0.0 copy-done
  124.5 1.1 select_bitcast_fusion
  125.6 0.0 copy-done.3
  125.6 0.7 select_bitcast_fusion.1
  126.4 12.0 %keep_part.1.base_ref = f32[256,4096]{1,0:T(8,128)} custom-call(s32[1]{0:T(128)} %bitcast.8.pick, bf16[192,1536]{1,0:T(8,128)(2,1)} %get-tuple-element.10.g_ref, bf16[6144,1536]{1,0:T(8,128)(2,1)} %all-gather.2.cloned.1.call-done.b_ref, f32[192,6144]{1,0:T(8,128)} %bitcast.17, s32[1,192]{1,0:T(1,128)} %get-tuple-element.15.rows_ref, ...), custom_call_target="tpu_custom_call" | custom-call | flops 5000000000 | bytes 10000000 | tf_op jit(solution)/shard_map/keep_part/pallas_call | solution.py:544
  138.4 0.0 collective-permute-done.1.s_ref
  138.4 0.8 copy-done.2
  139.2 4.0 %join_part.2.base_ref = f32[256,4096]{1,0:T(8,128)} custom-call(bf16[192,1536]{1,0:T(8,128)(2,1)} %copy-done.2, s32[1,192]{1,0:T(1,128)} %get-tuple-element.16.rows_ref, s32[8,1,384]{2,1,0:T(1,128)} %get-tuple-element.18.cols_ref, f32[256,4096]{1,0:T(8,128)} %keep_part.1.base_ref), custom_call_target="tpu_custom_call", output_to_operand_aliasing={{}: (3, {})} | custom-call | flops 1000000000 | bytes 10000000 | tf_op jit(solution)/shard_map/join_part/pallas_call | solution.py:574
  143.1 2.6 %collective-permute-done.s_ref = bf16[192,1536]{1,0:T(8,128)(2,1)S(1)} collective-permute-done((bf16[192,1536]{1,0:T(8,128)(2,1)}, bf16[192,1536]{1,0:T(8,128)(2,1)S(1)}, u32[]{:S(2)}, u32[]{:S(2)}) %collective-permute-start) | collective-permute-done | bytes 589856 | tf_op jit(solution)/shard_map/ppermute | solution.py:631
  145.7 0.8 copy-done.1
  146.6 3.9 %join_part.3 = f32[256,4096]{1,0:T(8,128)} custom-call(bf16[192,1536]{1,0:T(8,128)(2,1)} %copy-done.1, s32[1,192]{1,0:T(1,128)} %get-tuple-element.16.rows_ref, s32[8,1,384]{2,1,0:T(1,128)} %get-tuple-element.18.cols_ref, f32[256,4096]{1,0:T(8,128)} %join_part.2.base_ref), custom_call_target="tpu_custom_call", output_to_operand_aliasing={{}: (3, {})} | custom-call | flops 1000000000 | bytes 10000000 | tf_op jit(solution)/shard_map/join_part/pallas_call | solution.py:574
  (4 shorter events, 0.0 us)
Async XLA Ops:
  7.2 106.7 %all-gather.2.cloned.1.call-start = ((), (), s32[]{:S(2)}) async-start(), calls=%async_computation | async-start | bytes 19464192 | tf_op jit(solution)/shard_map/all_gather | solution.py:614
  118.4 19.9 %collective-permute-start.1 = (bf16[192,1536]{1,0:T(8,128)(2,1)}, bf16[192,1536]{1,0:T(8,128)(2,1)S(1)}, u32[]{:S(2)}, u32[]{:S(2)}) collective-permute-start(bf16[192,1536]{1,0:T(8,128)(2,1)} %send_part.2), channel_id=1, source_target_pairs={{0,32},{1,33},{2,34},{3,35},{4,36},{5,37},{6,38},{7,39},{8,40},{9,... | collective-permute-start | bytes 1769480 | tf_op jit(solution)/shard_map/ppermute | solution.py:631
  119.7 4.8 %copy-start = (f32[192,1536]{1,0:T(8,128)S(1)}, f32[192,1536]{1,0:T(8,128)}, u32[]{:S(2)}) copy-start(f32[192,1536]{1,0:T(8,128)} %get-tuple-element.12) | copy-start | bytes 3538948
  124.4 1.3 copy-start.3
  124.4 21.4 %collective-permute-start = (bf16[192,1536]{1,0:T(8,128)(2,1)}, bf16[192,1536]{1,0:T(8,128)(2,1)S(1)}, u32[]{:S(2)}, u32[]{:S(2)}) collective-permute-start(bf16[192,1536]{1,0:T(8,128)(2,1)} %send_part.3), channel_id=1, source_target_pairs={{0,32},{1,33},{2,34},{3,35},{4,36},{5,37},{6,38},{7,39},{8,40},{9,... | collective-permute-start | bytes 1769480 | tf_op jit(solution)/shard_map/ppermute | solution.py:631
  138.4 0.8 copy-start.2
  145.7 0.8 copy-start.1
Sparse Core Ops, SparseCore 0:
  10.8 95.6 all-gather.1
